TPU v7x, 32 devices: a whole 2x2x4 slice. The times are simulated.
32 devices in a mesh: groups: 2 (over y), gx: 16 (over z, x, core).
Axes of the slice: x: 2, y: 2, z: 4, core: 2. Of those that a mesh axis runs over, the one named last changes fastest.
Arguments:
- features: float32 [48, 64, 96, 128], P(None, ('groups', 'gx')), parts along dimension 1, may hold values from -6 to 6
- fine_weights: bfloat16 [1536, 8, 48, 48], P('gx'), may hold values from -1.796875 to 1.796875
- middle_weights: bfloat16 [384, 4, 48, 48], P('gx'), may hold values from -3 to 3
- lift_fine: float32 [48, 48], replicated, may hold values from -0.875 to 0.875
- lift_middle: float32 [48, 48], replicated, may hold values from -0.875 to 0.875
- project_out: float32 [48, 48], replicated, may hold values from -0.875 to 0.875
Outputs:
- result: float32 [48, 64, 96, 128], P(None, ('groups', 'gx')), parts along dimension 1
There are 2 independent parts, one for each index of `groups`. A program takes and returns all parts, laid end to end along the dimension named above; an argument that names none is the same for every part. Nothing has to cross between parts.
All inputs are finite; a program needn't handle non-finite values.
Results may differ from a plain program's by a relative error of at most 0.0018.
Values sent between devices are 32-bit elements; how exact they have to be, the bound alone decides.
A program may use at most 128 MiB of HBM per device.

v0:
```python
import functools

import jax
import jax.numpy as jnp
import numpy as np
from jax import lax
from jax.experimental import pallas as pl
from jax.experimental.pallas import tpu as pltpu
from jax.sharding import PartitionSpec as P

KY = 48
KZ = 32


HIGHEST = lax.Precision.HIGHEST


def cosine_table(modes_kept, length, columns):
    orders = jnp.arange(modes_kept, dtype=jnp.int32)[:, None]
    points = jnp.arange(columns, dtype=jnp.int32)[None, :]
    phase = orders * (2 * points + 1) % (4 * length)
    angle = jnp.pi / (2 * length) * phase.astype(jnp.float32)
    scales = jnp.where(
        orders == 0, jnp.sqrt(jnp.float32(1.0 / length)), jnp.sqrt(jnp.float32(2.0 / length))
    )
    return scales * jnp.cos(angle)


def forward_yz(values, modes_y, modes_z):
    channels, local_x, cells_y, cells_z = values.shape
    table_z = cosine_table(modes_z, cells_z, cells_z)
    table_y = cosine_table(modes_y, cells_y, cells_y)
    along_z = jnp.einsum("cxyz,jz->cxyj", values, table_z, precision=HIGHEST)
    both = jnp.einsum("cxyj,iy->ijxc", along_z, table_y, precision=HIGHEST)
    return both.reshape(modes_y * modes_z, local_x, channels)


def inverse_yz(coeffs, modes_y, modes_z, cells_y, cells_z):
    total, local_x, channels = coeffs.shape
    shaped = coeffs.reshape(modes_y, modes_z, local_x, channels)
    table_z = cosine_table(modes_z, cells_z, cells_z)
    table_y = cosine_table(modes_y, cells_y, cells_y)
    along_y = jnp.einsum("ijxc,iy->jxcy", shaped, table_y, precision=HIGHEST)
    return jnp.einsum("jxcy,jz->cxyz", along_y, table_z, precision=HIGHEST)


def mix_modes(modal, weights):
    return jnp.einsum(
        "mkc,mkco->mko", modal.astype(jnp.bfloat16), weights, preferred_element_type=jnp.float32
    )


def pointwise(values, matrix):
    return jnp.einsum("cxyz,co->oxyz", values, matrix, precision=HIGHEST)


def coarsen(values):
    channels, cells_x, cells_y, cells_z = values.shape
    shaped = values.reshape(channels, cells_x // 2, 2, cells_y // 2, 2, cells_z // 2, 2)
    return jnp.mean(shaped, axis=(2, 4, 6))


def refine(values):
    return jnp.repeat(jnp.repeat(jnp.repeat(values, 2, axis=1), 2, axis=2), 2, axis=3)


def general_device(features, fine_weights, middle_weights, lift_fine, lift_middle, project_out):
    channels, local_x, cells_y, cells_z = features.shape
    group_size = lax.axis_size("gx")
    cells_x = local_x * group_size
    modes_x = fine_weights.shape[1]
    coeffs = forward_yz(features, KY, KZ)
    table_x = cosine_table(modes_x, cells_x, cells_x)
    owned_pairs = coeffs.shape[0] // group_size
    grouped = coeffs.reshape(group_size, owned_pairs, local_x, channels)
    modal = jnp.einsum(
        "amxc,kx->mkc",
        lax.all_to_all(grouped, "gx", split_axis=0, concat_axis=2, tiled=True),
        table_x,
        precision=HIGHEST,
    )
    mixed = mix_modes(modal, fine_weights)
    back = jnp.einsum("mkc,kx->mxc", mixed, table_x, precision=HIGHEST)
    slabs = lax.all_to_all(back, "gx", split_axis=1, concat_axis=0, tiled=True)
    level_one = jax.nn.gelu(
        inverse_yz(slabs, KY, KZ, cells_y, cells_z) + pointwise(features, lift_fine),
        approximate=False,
    )
    pooled = coarsen(level_one)
    half_x = local_x // 2
    half_ky = KY // 2
    half_kz = KZ // 2
    half_modes = middle_weights.shape[1]
    coarse_x = half_x * group_size
    coarse_coeffs = forward_yz(pooled, half_ky, half_kz)
    coarse_pencils = lax.all_to_all(coarse_coeffs, "gx", split_axis=0, concat_axis=1, tiled=True)
    coarse_table = cosine_table(half_modes, coarse_x, coarse_x)
    coarse_modal = jnp.einsum("mxc,kx->mkc", coarse_pencils, coarse_table, precision=HIGHEST)
    coarse_mixed = mix_modes(coarse_modal, middle_weights)
    coarse_back = jnp.einsum("mkc,kx->mxc", coarse_mixed, coarse_table, precision=HIGHEST)
    coarse_slabs = lax.all_to_all(coarse_back, "gx", split_axis=1, concat_axis=0, tiled=True)
    level_two = jax.nn.gelu(
        inverse_yz(coarse_slabs, half_ky, half_kz, cells_y // 2, cells_z // 2)
        + pointwise(pooled, lift_middle),
        approximate=False,
    )
    return features + pointwise(level_one + refine(level_two), project_out)


BF16 = jnp.bfloat16
F32 = jnp.float32


def host_table(modes_kept, length):
    orders = np.arange(modes_kept)[:, None]
    points = np.arange(length)[None, :]
    scales = np.where(orders == 0, np.sqrt(1.0 / length), np.sqrt(2.0 / length))
    return scales * np.cos(np.pi * orders * (2 * points + 1) / (2 * length))


def host_split(table):
    table = np.asarray(table, np.float32)
    high = table.astype(jnp.bfloat16)
    low = (table - high.astype(np.float32)).astype(jnp.bfloat16)
    return high, low


def left_rows(table):
    high, low = host_split(table)
    return jnp.asarray(
        np.concatenate([np.concatenate([high, high], 1), np.concatenate([low, low], 1)], 0)
    )


def left_three(table):
    high, low = host_split(table)
    return jnp.asarray(np.concatenate([high, high, low], 1))


def right_three(table):
    high, low = host_split(table)
    return jnp.asarray(np.concatenate([high, high, low], 0))


def split(values):
    high = values.astype(BF16)
    low = (values - high.astype(F32)).astype(BF16)
    return high, low


def dot(left, right):
    return jnp.dot(left, right, preferred_element_type=F32)


def dot_left3(left3, values):
    high, low = split(values)
    return dot(left3, jnp.concatenate([high, low, high], 0))


def dot_right3(values, right3):
    high, low = split(values)
    return dot(jnp.concatenate([high, low, high], 1), right3)


def gelu(t):
    return 0.5 * t * (1.0 + lax.erf(t * np.float32(np.sqrt(0.5))))


def whole():
    return pl.BlockSpec(memory_space=pltpu.VMEM)


def forward_kernel(rows_per_mode, f_ref, ty_ref, tz_ref, out_ref):
    step = pl.program_id(0)
    per_row, local_x, cells_y, cells_z = f_ref.shape
    modes = ty_ref.shape[0] // 2
    width = 128 // per_row
    lane = lax.broadcasted_iota(jnp.int32, (modes, 128), 1) // width
    total = [jnp.zeros((modes, 128), F32) for _ in range(local_x)]
    for c in range(per_row):
        wide = jnp.concatenate([f_ref[c, x] for x in range(local_x)], 1)
        high, low = split(wide)
        both = dot(ty_ref[...], jnp.concatenate([high, low], 0))
        both = both[:modes] + both[modes:]
        stacked = jnp.concatenate(
            [both[:, x * cells_z : (x + 1) * cells_z] for x in range(local_x)], 0
        )
        done = dot_right3(stacked, tz_ref[...])
        for x in range(local_x):
            total[x] = jnp.where(lane == c, done[x * modes : (x + 1) * modes], total[x])
    chunks = rows_per_mode // local_x
    for x in range(local_x):
        out_ref[pl.ds(x * chunks + step, modes, stride=rows_per_mode), :] = total[x]


def forward_fine(features, modes_y, modes_z):
    channels, local_x, cells_y, cells_z = features.shape
    per_row = 128 // modes_z
    chunks = channels // per_row
    rows = modes_y * local_x * chunks
    ty = left_rows(host_table(modes_y, cells_y))
    tz = right_three(np.tile(host_table(modes_z, cells_z).T, (1, per_row)))
    return pl.pallas_call(
        functools.partial(forward_kernel, local_x * chunks),
        grid=(chunks,),
        out_shape=jax.ShapeDtypeStruct((rows, 128), F32),
        in_specs=[
            pl.BlockSpec((per_row, local_x, cells_y, cells_z), lambda h: (h, 0, 0, 0)),
            pl.BlockSpec(ty.shape, lambda h: (0, 0)),
            pl.BlockSpec(tz.shape, lambda h: (0, 0)),
        ],
        out_specs=pl.BlockSpec((rows, 128), lambda h: (0, 0)),
        name="forward_fine",
    )(features, ty, tz)


def middle_kernel(
    slab_ref, f_ref, ty_ref, tz_ref, lift_ref, proj_ref, yc_ref, zc_ref, zp_ref,
    base_ref, pooled_ref, coarse_ref, spec_ref, sum_ref,
):
    channels, local_x, cells_y, cells_z = f_ref.shape
    modes_y = ty_ref.shape[1] // 3
    rows_per_mode = slab_ref.shape[0] // modes_y
    chunks = rows_per_mode // local_x
    per_row = channels // chunks
    width = 128 // per_row
    lane = lax.broadcasted_iota(jnp.int32, (local_x * cells_y, 128), 1) // width

    def inverse(h, carry):
        wide = jnp.concatenate(
            [slab_ref[pl.ds(x * chunks + h, modes_y, stride=rows_per_mode), :] for x in range(local_x)], 1
        )
        grown = dot_left3(ty_ref[...], wide)
        stacked = jnp.concatenate([grown[:, x * 128 : (x + 1) * 128] for x in range(local_x)], 0)
        high, low = split(stacked)
        left = jnp.concatenate([high, low, high], 1)
        lanes = jnp.concatenate([lane] * 3, 1)
        for c in range(per_row):
            masked = jnp.where(lanes == c, left, jnp.zeros_like(left))
            done = dot(masked, tz_ref[...])
            for x in range(local_x):
                spec_ref[h * per_row + c, x] = done[x * cells_y : (x + 1) * cells_y]
        return carry

    lax.fori_loop(0, chunks, inverse, 0)

    def block(b, carry):
        at = pl.ds(pl.multiple_of(b * 8, 8), 8)
        values = jnp.concatenate(
            [f_ref[:, x, at, :].reshape(channels * 8, cells_z) for x in range(local_x)], 1
        )
        spectral = jnp.concatenate(
            [spec_ref[:, x, at, :].reshape(channels * 8, cells_z) for x in range(local_x)], 1
        )
        level = gelu(dot_left3(lift_ref[...], values) + spectral)
        base = values + dot_left3(proj_ref[...], level)
        for x in range(local_x):
            base_ref[:, x, at, :] = base[:, x * cells_z : (x + 1) * cells_z].reshape(channels, 8, cells_z)
        sum_ref[:, at, :] = (level[:, :cells_z] + level[:, cells_z:]).reshape(channels, 8, cells_z)
        return carry

    lax.fori_loop(0, cells_y // 8, block, 0)

    half_y = cells_y // 2
    modes_c = yc_ref.shape[0] // 2 - half_y
    parts = zc_ref.shape[1] // 128
    coarse_chunks = coarse_ref.shape[0] // (modes_c * parts)
    coarse_per = channels // coarse_chunks
    coarse_lane = (
        lax.broadcasted_iota(jnp.int32, (modes_c, parts * 128), 1) // (128 // coarse_per) % coarse_per
    )
    rows = modes_c + half_y

    def coarse(h, carry):
        total = jnp.zeros((modes_c, parts * 128), F32)
        for pair in range(coarse_per // 2):
            first = h * coarse_per + pair * 2
            wide = jnp.concatenate([sum_ref[first], sum_ref[first + 1]], 1)
            high, low = split(wide)
            both = dot(yc_ref[...], jnp.concatenate([high, low], 0))
            both = both[:rows] + both[rows:]
            modal = jnp.concatenate([both[half_y:, :128], both[half_y:, 128:]], 0)
            done = dot_right3(modal, zc_ref[...])
            for k in range(2):
                total = jnp.where(
                    coarse_lane == pair * 2 + k, done[k * modes_c : (k + 1) * modes_c], total
                )
            flat = jnp.concatenate([both[:half_y, :128], both[:half_y, 128:]], 0)
            high, low = split(flat)
            mean = dot(jnp.concatenate([high, low], 1), zp_ref[...])
            pooled_ref[first] = mean[:half_y]
            pooled_ref[first + 1] = mean[half_y:]
        for p in range(parts):
            coarse_ref[pl.ds(p * coarse_chunks + h, modes_c, stride=parts * coarse_chunks), :] = total[
                :, p * 128 : (p + 1) * 128
            ]
        return carry

    lax.fori_loop(0, coarse_chunks, coarse, 0)


def blockwise(matrix, left):
    high = matrix.astype(BF16)
    low = (matrix - lax.optimization_barrier(high).astype(F32)).astype(BF16)
    out = []
    for part in (high, high, low):
        grown = part.T[:, None, :, None] * jnp.asarray(left, BF16)[None, :, None, :]
        out.append(grown.reshape(matrix.shape[1] * left.shape[0], matrix.shape[0] * left.shape[1]))
    return jnp.concatenate(out, 1)


def final_kernel(
    slab_ref, pooled_ref, base_ref, ty_ref, tz_ref, lift_ref, proj_ref, out_ref, spec_ref
):
    channels, half_y, _ = pooled_ref.shape
    local_x = base_ref.shape[1]
    modes = ty_ref.shape[1] // 3
    rows_per_mode = slab_ref.shape[0] // modes
    parts = tz_ref.shape[0] // (3 * 128)
    chunks = rows_per_mode // parts
    per_row = channels // chunks
    stacked = []
    for h in range(chunks):
        wide = jnp.concatenate(
            [slab_ref[pl.ds(p * chunks + h, modes, stride=rows_per_mode), :] for p in range(parts)], 1
        )
        stacked.append(dot_left3(ty_ref[...], wide))
    grown = jnp.concatenate(stacked, 0)
    high, low = split(grown)
    left = jnp.concatenate([high, low, high], 1)
    lane = lax.broadcasted_iota(jnp.int32, left.shape, 1) // (128 // per_row) % per_row

    for c in range(per_row):
        done = dot(jnp.where(lane == c, left, jnp.zeros_like(left)), tz_ref[...])
        for h in range(chunks):
            spec_ref[h * per_row + c] = done[h * half_y : (h + 1) * half_y]

    def block(g, carry):
        at = [pl.ds(pl.multiple_of(g * 16 + 8 * k, 8), 8) for k in range(2)]
        pooled = jnp.concatenate([pooled_ref[:, a, :].reshape(channels * 8, 128) for a in at], 1)
        spectral = jnp.concatenate([spec_ref[:, a, :].reshape(channels * 8, 128) for a in at], 1)
        level = gelu(dot_left3(lift_ref[...], pooled) + spectral)
        added = dot_left3(proj_ref[...], level)
        for k in range(2):
            for b in range(2):
                piece = added[b * channels * 8 : (b + 1) * channels * 8, k * 128 : (k + 1) * 128]
                piece = piece.reshape(channels, 8, 128)
                rows = pl.ds(pl.multiple_of(g * 32 + 16 * k + 8 * b, 8), 8)
                for x in range(local_x):
                    out_ref[:, x, rows, :] = base_ref[:, x, rows, :] + piece
        return carry

    lax.fori_loop(0, half_y // 16, block, 0)


def exchange(values, axis_size):
    rows = values.shape[0] // axis_size
    flat = values.reshape(axis_size, rows, 128)
    return lax.all_to_all(flat, "gx", split_axis=0, concat_axis=0, tiled=True)


def on_device(features, fine_weights, middle_weights, lift_fine, lift_middle, project_out):
    channels, local_x, cells_y, cells_z = features.shape
    n = lax.axis_size("gx")
    owned = fine_weights.shape[0]
    owned_c = middle_weights.shape[0]
    half_ky, half_kz = KY // 2, KZ // 2
    narrow = 8
    fits = (
        owned % KZ == 0
        and owned_c % narrow == 0
        and local_x == 2
        and cells_z == 128
        and cells_y % 32 == 0
        and channels % 16 == 0
    )
    if not fits:
        return general_device(
            features, fine_weights, middle_weights, lift_fine, lift_middle, project_out
        )
    modes_x = fine_weights.shape[1]
    modes_c = middle_weights.shape[1]
    per_row = 128 // KZ
    chunks = channels // per_row
    tx = jnp.asarray(host_table(modes_x, local_x * n), F32).reshape(modes_x, n, local_x)
    txc = jnp.asarray(host_table(modes_c, n), F32)
    lift = blockwise(lift_fine, np.eye(8))
    proj = blockwise(project_out, np.eye(8))
    liftm = blockwise(lift_middle, np.eye(8))
    spread = np.repeat(np.eye(8), 2, axis=0)
    projm = jnp.concatenate(
        [blockwise(project_out, spread[8 * b : 8 * b + 8]) for b in range(2)], 0
    )

    coeffs = forward_fine(features, KY, KZ)
    got = exchange(coeffs, n)
    got = got.reshape(n, owned // KZ, local_x, channels, KZ)
    modal = jnp.einsum("aixcj,kax->ijkc", got, tx, precision=HIGHEST)
    modal = modal.reshape(owned, modes_x, channels)
    mixed = mix_modes(modal, fine_weights).reshape(owned // KZ, KZ, modes_x, channels)
    back = jnp.einsum("ijko,kax->aixoj", mixed, tx, precision=HIGHEST)
    slab = exchange(back.reshape(-1, 128), n).reshape(-1, 128)

    half_y, half_z = cells_y // 2, cells_z // 2
    pool_y = np.repeat(np.eye(half_y), 2, axis=1) * 0.5
    pool_z = np.repeat(np.eye(half_z), 2, axis=1) * 0.25
    ty_c = host_table(half_ky, half_y)
    tz_c = host_table(half_kz, half_z)
    parts = half_kz // narrow
    per_c = 128 // narrow
    chunks_c = channels // per_c
    yc = left_rows(np.concatenate([pool_y, ty_c @ pool_y], 0))
    zc_full = (tz_c @ pool_z).T.reshape(cells_z, parts, 1, narrow)
    zc = right_three(np.broadcast_to(zc_full, (cells_z, parts, per_c, narrow)).reshape(cells_z, -1))
    zp = np.repeat(pool_z, 2, axis=0).T
    zp = np.asarray(zp, jnp.bfloat16)
    zp = jnp.asarray(np.concatenate([zp, zp], 0))
    ty_i = left_three(host_table(KY, cells_y).T)
    tz_i = right_three(np.tile(host_table(KZ, cells_z), (per_row, 1)))
    base, pooled, coarse = pl.pallas_call(
        middle_kernel,
        out_shape=(
            jax.ShapeDtypeStruct(features.shape, F32),
            jax.ShapeDtypeStruct((channels, half_y, 128), F32),
            jax.ShapeDtypeStruct((half_ky * parts * chunks_c, 128), F32),
        ),
        in_specs=[whole()] * 9,
        out_specs=(whole(), whole(), whole()),
        scratch_shapes=[
            pltpu.VMEM(features.shape, F32),
            pltpu.VMEM((channels, cells_y, cells_z), F32),
        ],
        name="middle",
    )(slab, features, ty_i, tz_i, lift, proj, yc, zc, zp)

    got = exchange(coarse, n).reshape(n, owned_c // narrow, chunks_c, per_c, narrow)
    modal = jnp.einsum("aqhlj,ka->qjkhl", got, txc, precision=HIGHEST)
    mixed = mix_modes(modal.reshape(owned_c, modes_c, channels), middle_weights)
    mixed = mixed.reshape(owned_c // narrow, narrow, modes_c, chunks_c, per_c)
    back = jnp.einsum("qjkhl,ka->aqhlj", mixed, txc, precision=HIGHEST)
    slab = exchange(back.reshape(-1, 128), n).reshape(-1, 128)

    tyc_i = left_three(ty_c.T)
    grown = np.repeat(tz_c, 2, axis=1).reshape(parts, 1, narrow, cells_z)
    tzc_i = right_three(np.broadcast_to(grown, (parts, per_c, narrow, cells_z)).reshape(-1, cells_z))
    return pl.pallas_call(
        final_kernel,
        out_shape=jax.ShapeDtypeStruct(features.shape, F32),
        in_specs=[whole()] * 7,
        out_specs=whole(),
        scratch_shapes=[pltpu.VMEM((channels, half_y, 128), F32)],
        name="final",
    )(slab, pooled, base, tyc_i, tzc_i, liftm, projm)


def solution(mesh):
    in_specs = (
        P(None, ("groups", "gx"), None, None),
        P("gx", None, None, None),
        P("gx", None, None, None),
        P(),
        P(),
        P(),
    )
    out_specs = P(None, ("groups", "gx"), None, None)
    return jax.shard_map(
        on_device, mesh=mesh, in_specs=in_specs, out_specs=out_specs, check_vma=False
    )
```

profile of v0, /device:TPU:0, one launch (start us, length us, event | category | flops | bytes accessed | tf_op | source)
XLA Modules:
  0.0 223.8 jit_solution(3161410137061331874)
XLA Ops:
  0.0 11.9 %forward_fine.1 = f32[1152,128]{1,0:T(8,128)} custom-call(f32[48,2,96,128]{3,2,1,0:T(8,128)} %f_ref.3, bf16[96,192]{1,0:T(8,128)(2,1)} %constant.33.clone.ty_ref, bf16[384,128]{1,0:T(8,128)(2,1)} %constant.34.clone.tz_ref), custom_call_target="tpu_custom_call" | custom-call | tf_op jit(solution)/shard_map/forward_fine/pallas_call | solution.py:203
  11.9 7.4 %all-to-all-start = ((f32[16,72,128]{2,1,0:T(8,128)}), f32[16,72,128]{2,1,0:T(8,128)}, u32[]{:S(2)}, u32[]{:S(2)}) async-start(f32[16,72,128]{2,1,0:T(8,128)} %bitcast.86), calls=%async_computation | async-start | bytes 1179648 | tf_op jit(solution)/shard_map/all_to_all | solution.py:359
  22.9 15.8 %copy.69 = bf16[96,8,48,48]{3,2,1,0:T(8,128)(2,1)} copy(bf16[96,8,48,48]{0,3,2,1:T(8,128)(2,1)} %param.33) | data formatting | bytes 7077888 | tf_op args[1]
  44.6 5.1 %fusion.2 = f32[96,8,1,48]{3,2,1,0:T(1,128)S(1)} fusion(bf16[96,8,48,48]{3,2,1,0:T(8,128)(2,1)} %copy.69, bf16[96,8,48,1]{2,1,0,3:T(8,128)(2,1)S(1)} %bitcast.88), kind=kOutput, calls=%fused_computation.20 | convolution fusion | flops 3538944 | bytes 3760128 | tf_op jit(solution)/shard_map/mkc,mkco->mko/dot_general | solution.py:48
  49.7 2.6 %convolution_bitcast_fusion = f32[16,3,2,48,32]{3,0,2,4,1:T(8,128)} fusion(f32[3,32,8,48,1]{3,2,4,1,0:T(8,128)S(1)} %bitcast.87, f32[8,16,2,1,1]{1,0,2,4,3:T(8,128)S(1)} %copy-done.5), kind=kOutput, calls=%fused_computation.11 | convolution fusion | flops 14155776 | bytes 738304 | tf_op jit(solution)/shard_map/ijko,kax->aixoj/dot_general | solution.py:401
  55.7 6.0 %all-to-all-start.1 = ((f32[16,72,128]{2,1,0:T(8,128)}), f32[16,72,128]{2,1,0:T(8,128)S(1)}, u32[]{:S(2)}, u32[]{:S(2)}) async-start(f32[16,72,128]{2,1,0:T(8,128)} %reshape_reshape.6), calls=%async_computation.1 | async-start | bytes 1179648 | tf_op jit(solution)/shard_map/all_to_all | solution.py:359
  61.6 16.6 %broadcast_multiply_fusion.2 = (bf16[48,8,48,8]{3,2,1,0:T(8,128)(2,1)}, bf16[48,8,48,8]{3,2,1,0:T(8,128)(2,1)}, bf16[48,8,48,8]{3,2,1,0:T(8,128)(2,1)}, bf16[48,...) fusion(bf16[8,8]{1,0:T(8,128)(2,1)} %constant.31.clone, ...), kind=kLoop, calls=%fused_computation.2 | loop fusion | flops 1474560 | bytes 2977152 | tf_op jit(solution)/shard_map/mul | solution.py:307
  78.3 6.4 %mul.240 = bf16[384,384]{1,0:T(8,128)(2,1)S(1)} reshape(bf16[48,8,48,8]{3,2,1,0:T(8,128)(2,1)} %get-tuple-element.23) | data formatting | bytes 589824 | tf_op jit(solution)/shard_map/mul | solution.py:307
  84.7 6.4 %mul.247 = bf16[384,384]{1,0:T(8,128)(2,1)S(1)} reshape(bf16[48,8,48,8]{3,2,1,0:T(8,128)(2,1)} %get-tuple-element.22) | data formatting | bytes 589824 | tf_op jit(solution)/shard_map/mul | solution.py:307
  91.1 7.1 %mul.251 = bf16[384,384]{1,0:T(8,128)(2,1)} reshape(bf16[48,8,48,8]{3,2,1,0:T(8,128)(2,1)} %get-tuple-element.17) | data formatting | bytes 589824 | tf_op jit(solution)/shard_map/mul | solution.py:307
  98.2 7.1 %mul.258 = bf16[384,384]{1,0:T(8,128)(2,1)} reshape(bf16[48,8,48,8]{3,2,1,0:T(8,128)(2,1)} %get-tuple-element.16) | data formatting | bytes 589824 | tf_op jit(solution)/shard_map/mul | solution.py:307
  105.3 6.4 %mul.272 = bf16[384,384]{1,0:T(8,128)(2,1)S(1)} reshape(bf16[48,8,48,8]{3,2,1,0:T(8,128)(2,1)} %get-tuple-element.19) | data formatting | bytes 589824 | tf_op jit(solution)/shard_map/mul | solution.py:307
  111.7 6.4 %mul.278 = bf16[384,384]{1,0:T(8,128)(2,1)S(1)} reshape(bf16[48,8,48,8]{3,2,1,0:T(8,128)(2,1)} %get-tuple-element.14) | data formatting | bytes 589824 | tf_op jit(solution)/shard_map/mul | solution.py:307
  118.1 6.6 %mul.281 = bf16[384,384]{1,0:T(8,128)(2,1)S(1)} reshape(bf16[48,8,48,8]{3,2,1,0:T(8,128)(2,1)} %get-tuple-element.18) | data formatting | bytes 589824 | tf_op jit(solution)/shard_map/mul | solution.py:307
  124.7 6.4 %mul.287 = bf16[384,384]{1,0:T(8,128)(2,1)S(1)} reshape(bf16[48,8,48,8]{3,2,1,0:T(8,128)(2,1)} %get-tuple-element.15) | data formatting | bytes 589824 | tf_op jit(solution)/shard_map/mul | solution.py:307
  131.1 2.5 %pad_maximum_fusion = (bf16[384,1152]{1,0:T(8,128)(2,1)}, bf16[384,1152]{1,0:T(8,128)(2,1)}) fusion(bf16[384,384]{1,0:T(8,128)(2,1)S(1)} %mul.247, bf16[384,384]{1,0:T(8,128)(2,1)S(1)} %mul.240, bf16[384,384]{1,0:T(8,128)(2,1)} %mul.258, bf16[384,384]{1,0:T(8,128)(2,1)} %mul.251), kind=kLoop, calls=%fused_computation.17 | loop fusion | flops 5308416 | bytes 2949120 | tf_op jit(solution)/shard_map/concatenate | solution.py:309
  134.5 30.0 %middle.1 = (f32[48,2,96,128]{3,2,1,0:T(8,128)}, f32[48,48,128]{2,1,0:T(8,128)}, f32[144,128]{1,0:T(8,128)}) custom-call(f32[1152,128]{1,0:T(8,128)} %bitcast.83, f32[48,2,96,128]{3,2,1,0:T(8,128)} %f_ref.3, bf16[96,144]{1,0:T(8,128)(2,1)} %constant.38.clone.ty_ref, bf16[384,128]{1,0:T(8,128)(2,1)} %constant.39.clone.tz_ref, ...), custom_call_target="tpu_custom_call" | custom-call | tf_op jit(solution)/shard_map/middle/pallas_call | solution.py:420
  166.0 6.0 %all-to-all-start.2 = ((f32[16,9,128]{2,1,0:T(8,128)}), f32[16,9,128]{2,1,0:T(8,128)S(1)}, u32[]{:S(2)}, u32[]{:S(2)}) async-start(f32[16,9,128]{2,1,0:T(8,128)} %reshape.117), calls=%async_computation.2 | async-start | bytes 262144 | tf_op jit(solution)/shard_map/all_to_all | solution.py:359
  173.4 6.4 %mul.262 = bf16[384,384]{1,0:T(8,128)(2,1)S(1)} reshape(bf16[48,8,48,8]{3,2,1,0:T(8,128)(2,1)} %get-tuple-element.20) | data formatting | bytes 589824 | tf_op jit(solution)/shard_map/mul | solution.py:307
  179.8 6.4 %mul.269 = bf16[384,384]{1,0:T(8,128)(2,1)S(1)} reshape(bf16[48,8,48,8]{3,2,1,0:T(8,128)(2,1)} %get-tuple-element.21) | data formatting | bytes 589824 | tf_op jit(solution)/shard_map/mul | solution.py:307
  186.5 7.8 %fusion.1 = bf16[3,8,4,3,16]{1,2,4,3,0:T(4,128)(2,1)S(1)} fusion(f32[16,3,3,16,8]{0,4,3,2,1:T(8,128)S(1)} %bitcast.84, f32[4,16,1,1,1]{1,0,4,3,2:T(4,128)S(1)} %copy-done.6), kind=kOutput, calls=%fused_computation.16 | convolution fusion | flops 889344 | bytes 83200 | tf_op jit(solution)/shard_map/aqhlj,ka->qjkhl/dot_general | solution.py:437
  197.5 6.0 %all-to-all-start.3 = ((f32[16,9,128]{2,1,0:T(8,128)}), f32[16,9,128]{2,1,0:T(8,128)S(1)}, u32[]{:S(2)}, u32[]{:S(2)}) async-start(f32[16,9,128]{2,1,0:T(8,128)} %copy.63), calls=%async_computation.3 | async-start | bytes 262144 | tf_op jit(solution)/shard_map/all_to_all | solution.py:359
  204.5 6.9 %all-to-all-done.3 = f32[16,9,128]{2,1,0:T(8,128)S(1)} async-done(((f32[16,9,128]{2,1,0:T(8,128)}), f32[16,9,128]{2,1,0:T(8,128)S(1)}, u32[]{:S(2)}, u32[]{:S(2)}) %all-to-all-start.3) | async-done | bytes 73760 | tf_op jit(solution)/shard_map/all_to_all | solution.py:359
  212.1 11.7 %final.1 = f32[48,2,96,128]{3,2,1,0:T(8,128)} custom-call(f32[144,128]{1,0:T(8,128)} %reshape.120.slab_ref, f32[48,48,128]{2,1,0:T(8,128)} %get-tuple-element.9.pooled_ref, f32[48,2,96,128]{3,2,1,0:T(8,128)} %get-tuple-element.10.base_ref, bf16[48,72]{1,0:T(8,128)(2,1)} %constant.40.clone.ty_ref, bf16[768,128]{1,0:T(8,128)(2,1)} %constant.41.clone.tz_ref, ...), custom_call_target="tpu_custom_call" | custom-call | tf_op jit(solution)/shard_map/final/pallas_call | solution.py:446
  (52 shorter events, 21.6 us)
Async XLA Ops:
  0.0 194.6 %copy-start = (bf16[24,4,48,48]{3,2,1,0:T(8,128)(2,1)S(1)}, bf16[24,4,48,48]{3,2,1,0:T(8,128)(2,1)}, u32[]{:S(2)}) copy-start(bf16[24,4,48,48]{3,2,1,0:T(8,128)(2,1)} %param.34) | copy-start | bytes 1327108
  0.0 19.3 %copy-start.2 = (f32[48,48]{1,0:T(8,128)S(1)}, f32[48,48]{1,0:T(8,128)}, u32[]{:S(2)}) copy-start(f32[48,48]{1,0:T(8,128)} %param.35) | copy-start | bytes 27652
  0.0 19.4 %copy-start.3 = (f32[48,48]{1,0:T(8,128)S(1)}, f32[48,48]{1,0:T(8,128)}, u32[]{:S(2)}) copy-start(f32[48,48]{1,0:T(8,128)} %param.37) | copy-start | bytes 27652
  0.0 20.2 %copy-start.4 = (f32[48,48]{1,0:T(8,128)S(1)}, f32[48,48]{1,0:T(8,128)}, u32[]{:S(2)}) copy-start(f32[48,48]{1,0:T(8,128)} %param.36) | copy-start | bytes 27652
  11.9 26.9 %all-to-all-start = ((f32[16,72,128]{2,1,0:T(8,128)}), f32[16,72,128]{2,1,0:T(8,128)}, u32[]{:S(2)}, u32[]{:S(2)}) async-start(f32[16,72,128]{2,1,0:T(8,128)} %bitcast.86), calls=%async_computation | async-start | bytes 1179648 | tf_op jit(solution)/shard_map/all_to_all | solution.py:359
  44.6 5.1 %copy-start.5 = (f32[8,16,2,1,1]{1,0,2,4,3:T(8,128)S(1)}, f32[8,16,2,1,1]{1,0,2,4,3:T(8,128)}, u32[]{:S(2)}) copy-start(f32[8,16,2,1,1]{1,0,2,4,3:T(8,128)} %constant.45) | copy-start | bytes 3076
  52.3 9.3 %copy-start.7 = (bf16[8,8]{1,0:T(8,128)(2,1)S(1)}, bf16[8,8]{1,0:T(8,128)(2,1)}, u32[]{:S(2)}) copy-start(bf16[8,8]{1,0:T(8,128)(2,1)} %constant.30.clone) | copy-start | bytes 388
  55.7 78.0 %all-to-all-start.1 = ((f32[16,72,128]{2,1,0:T(8,128)}), f32[16,72,128]{2,1,0:T(8,128)S(1)}, u32[]{:S(2)}, u32[]{:S(2)}) async-start(f32[16,72,128]{2,1,0:T(8,128)} %reshape_reshape.6), calls=%async_computation.1 | async-start | bytes 1179648 | tf_op jit(solution)/shard_map/all_to_all | solution.py:359
  133.6 0.8 copy-start.1
  166.0 20.2 %all-to-all-start.2 = ((f32[16,9,128]{2,1,0:T(8,128)}), f32[16,9,128]{2,1,0:T(8,128)S(1)}, u32[]{:S(2)}, u32[]{:S(2)}) async-start(f32[16,9,128]{2,1,0:T(8,128)} %reshape.117), calls=%async_computation.2 | async-start | bytes 262144 | tf_op jit(solution)/shard_map/all_to_all | solution.py:359
  179.8 6.7 %copy-start.6 = (f32[4,16,1,1,1]{1,0,4,3,2:T(4,128)S(1)}, f32[4,16,1,1,1]{1,0,4,3,2:T(4,128)}, u32[]{:S(2)}) copy-start(f32[4,16,1,1,1]{1,0,4,3,2:T(4,128)} %constant.46) | copy-start | bytes 772
  197.5 13.9 %all-to-all-start.3 = ((f32[16,9,128]{2,1,0:T(8,128)}), f32[16,9,128]{2,1,0:T(8,128)S(1)}, u32[]{:S(2)}, u32[]{:S(2)}) async-start(f32[16,9,128]{2,1,0:T(8,128)} %copy.63), calls=%async_computation.3 | async-start | bytes 262144 | tf_op jit(solution)/shard_map/all_to_all | solution.py:359
where the time goes:
time: 226 us; the launch traced here: 224 us
  local copies, waits for them, and re-layouts  96.6 us (43%)
  Pallas kernels  53.6 us (24%)
  starting transfers between devices  25.4 us (11%)
  other arithmetic  21.6 us (10%)
  matrix products  19.4 us (9%)
  waiting for transfers between devices  6.91 us (3%)
    mul x10, local copies, waits for them, and re-layouts, blockwise(): grown = part.T[:, None, :, None] * jnp.asarray(left, BF16)[None, :, None, :]  65.6 us
    pallas_call x1, Pallas kernels, on_device(): pl.pallas_call(middle_kernel, out_shape=(jax.ShapeDtypeStruct(features.sh...  30 us
    all_to_all x4, starting transfers between devices, exchange(): return lax.all_to_all(flat, 'gx', split_axis=0, concat_axis=0, tiled=True)  25.4 us
    unnamed x17, local copies, waits for them, and re-layouts  16.7 us
    mul x1, other arithmetic, blockwise(): grown = part.T[:, None, :, None] * jnp.asarray(left, BF16)[None, :, None, :]  16.6 us
    pallas_call x1, Pallas kernels, forward_fine(): pl.pallas_call(functools.partial(forward_kernel, local_x * chunks), grid=...  11.9 us
    pallas_call x1, Pallas kernels, on_device(): pl.pallas_call(final_kernel, out_shape=jax.ShapeDtypeStruct(features.shap...  11.7 us
    dot_general x1, matrix products, on_device(): modal = jnp.einsum('aqhlj,ka->qjkhl', got, txc, precision=HIGHEST)  7.84 us
  transfers between devices with their start and end apart: 4, of which 1 were waited for; matrix products, arithmetic and copies ran while one was open for 48% of the time, Pallas kernels for 0%

commit v1 on v0

--- a/solution.py
+++ b/solution.py
@@ -108,6 +108,7 @@
 
 
 BF16 = jnp.bfloat16
+MESH = pl.DeviceIdType.MESH
 F32 = jnp.float32
 
 
@@ -170,79 +171,96 @@
     return pl.BlockSpec(memory_space=pltpu.VMEM)
 
 
-def forward_kernel(rows_per_mode, f_ref, ty_ref, tz_ref, out_ref):
+def forward_kernel(f_ref, ty_ref, tz_ref, out_ref, grown_ref):
     step = pl.program_id(0)
-    per_row, local_x, cells_y, cells_z = f_ref.shape
+    block, local_x, cells_y, cells_z = f_ref.shape
     modes = ty_ref.shape[0] // 2
-    width = 128 // per_row
-    lane = lax.broadcasted_iota(jnp.int32, (modes, 128), 1) // width
-    total = [jnp.zeros((modes, 128), F32) for _ in range(local_x)]
-    for c in range(per_row):
+    n = out_ref.shape[0]
+    per = modes // n
+    rows = grown_ref.shape[0] // modes
+    channels = rows // local_x
+    half = channels // 2
+    for c in range(block):
         wide = jnp.concatenate([f_ref[c, x] for x in range(local_x)], 1)
         high, low = split(wide)
         both = dot(ty_ref[...], jnp.concatenate([high, low], 0))
         both = both[:modes] + both[modes:]
-        stacked = jnp.concatenate(
-            [both[:, x * cells_z : (x + 1) * cells_z] for x in range(local_x)], 0
-        )
-        done = dot_right3(stacked, tz_ref[...])
         for x in range(local_x):
-            total[x] = jnp.where(lane == c, done[x * modes : (x + 1) * modes], total[x])
-    chunks = rows_per_mode // local_x
-    for x in range(local_x):
-        out_ref[pl.ds(x * chunks + step, modes, stride=rows_per_mode), :] = total[x]
-
-
-def forward_fine(features, modes_y, modes_z):
+            grown_ref[pl.ds(x * channels + step * block + c, modes, stride=rows), :] = both[
+                :, x * cells_z : (x + 1) * cells_z
+            ]
+
+    @pl.when(step == pl.num_programs(0) - 1)
+    def _():
+        lane = lax.broadcasted_iota(jnp.int32, (3 * half, 128), 1) // 32
+
+        def owner(a, carry):
+            at = pl.multiple_of(a * per * rows, 8)
+            done = dot_right3(grown_ref[pl.ds(at, per * rows), :], tz_ref[...])
+            total = jnp.concatenate([done[g * rows + 3 * half : (g + 1) * rows] for g in range(per)], 0)
+            for g in range(per):
+                total = jnp.where(lane == g, done[g * rows : g * rows + 3 * half], total)
+            out_ref[a] = total
+            return carry
+
+        lax.fori_loop(0, n, owner, 0)
+
+
+def forward_fine(features, modes_y, modes_z, n):
     channels, local_x, cells_y, cells_z = features.shape
-    per_row = 128 // modes_z
-    chunks = channels // per_row
-    rows = modes_y * local_x * chunks
+    block = 4
     ty = left_rows(host_table(modes_y, cells_y))
-    tz = right_three(np.tile(host_table(modes_z, cells_z).T, (1, per_row)))
+    tz = right_three(np.tile(host_table(modes_z, cells_z).T, (1, 4)))
+    shape = (n, modes_y // n * channels // 2, 128)
     return pl.pallas_call(
-        functools.partial(forward_kernel, local_x * chunks),
-        grid=(chunks,),
-        out_shape=jax.ShapeDtypeStruct((rows, 128), F32),
+        forward_kernel,
+        grid=(channels // block,),
+        out_shape=jax.ShapeDtypeStruct(shape, F32),
         in_specs=[
-            pl.BlockSpec((per_row, local_x, cells_y, cells_z), lambda h: (h, 0, 0, 0)),
+            pl.BlockSpec((block, local_x, cells_y, cells_z), lambda h: (h, 0, 0, 0)),
             pl.BlockSpec(ty.shape, lambda h: (0, 0)),
             pl.BlockSpec(tz.shape, lambda h: (0, 0)),
         ],
-        out_specs=pl.BlockSpec((rows, 128), lambda h: (0, 0)),
+        out_specs=pl.BlockSpec(shape, lambda h: (0, 0, 0)),
+        scratch_shapes=[pltpu.VMEM((modes_y * local_x * channels, cells_z), F32)],
         name="forward_fine",
     )(features, ty, tz)
 
 
 def middle_kernel(
     slab_ref, f_ref, ty_ref, tz_ref, lift_ref, proj_ref, yc_ref, zc_ref, zp_ref,
-    base_ref, pooled_ref, coarse_ref, spec_ref, sum_ref,
+    base_ref, pooled_ref, coarse_ref, spec_ref, sum_ref, grown_ref,
 ):
     channels, local_x, cells_y, cells_z = f_ref.shape
     modes_y = ty_ref.shape[1] // 3
-    rows_per_mode = slab_ref.shape[0] // modes_y
-    chunks = rows_per_mode // local_x
-    per_row = channels // chunks
-    width = 128 // per_row
-    lane = lax.broadcasted_iota(jnp.int32, (local_x * cells_y, 128), 1) // width
-
-    def inverse(h, carry):
+    n = slab_ref.shape[0]
+    per = modes_y // n
+    half = channels // 2
+    rows = 2 * channels
+    lane = lax.broadcasted_iota(jnp.int32, (rows, 128), 1) // 32
+    tail = lax.broadcasted_iota(jnp.int32, (rows, 128), 0) >= 3 * half
+
+    def inverse(a, carry):
+        lefts = []
+        for g in range(per):
+            value = jnp.concatenate([slab_ref[a], slab_ref[a, g * half : (g + 1) * half]], 0)
+            lefts.append(jnp.where(lane == jnp.where(tail, 3, g), value, 0.0))
+        done = dot_right3(jnp.concatenate(lefts, 0), tz_ref[...])
+        grown_ref[pl.ds(pl.multiple_of(a * per * rows, 8), per * rows), :] = done
+        return carry
+
+    lax.fori_loop(0, n, inverse, 0)
+
+    def inverse_y(o, carry):
         wide = jnp.concatenate(
-            [slab_ref[pl.ds(x * chunks + h, modes_y, stride=rows_per_mode), :] for x in range(local_x)], 1
+            [grown_ref[pl.ds(x * channels + o, modes_y, stride=rows), :] for x in range(local_x)], 1
         )
-        grown = dot_left3(ty_ref[...], wide)
-        stacked = jnp.concatenate([grown[:, x * 128 : (x + 1) * 128] for x in range(local_x)], 0)
-        high, low = split(stacked)
-        left = jnp.concatenate([high, low, high], 1)
-        lanes = jnp.concatenate([lane] * 3, 1)
-        for c in range(per_row):
-            masked = jnp.where(lanes == c, left, jnp.zeros_like(left))
-            done = dot(masked, tz_ref[...])
-            for x in range(local_x):
-                spec_ref[h * per_row + c, x] = done[x * cells_y : (x + 1) * cells_y]
+        done = dot_left3(ty_ref[...], wide)
+        for x in range(local_x):
+            spec_ref[o, x] = done[:, x * cells_z : (x + 1) * cells_z]
         return carry
 
-    lax.fori_loop(0, chunks, inverse, 0)
+    lax.fori_loop(0, channels, inverse_y, 0, unroll=4)
 
     def block(b, carry):
         at = pl.ds(pl.multiple_of(b * 8, 8), 8)
@@ -299,14 +317,157 @@
     lax.fori_loop(0, coarse_chunks, coarse, 0)
 
 
-def blockwise(matrix, left):
-    high = matrix.astype(BF16)
-    low = (matrix - lax.optimization_barrier(high).astype(F32)).astype(BF16)
-    out = []
-    for part in (high, high, low):
-        grown = part.T[:, None, :, None] * jnp.asarray(left, BF16)[None, :, None, :]
-        out.append(grown.reshape(matrix.shape[1] * left.shape[0], matrix.shape[0] * left.shape[1]))
-    return jnp.concatenate(out, 1)
+def prepare_kernel(lift_ref, middle_ref, out_ref, lift_wide, middle_wide, proj_wide, final_wide):
+    channels = lift_ref.shape[0]
+    size = channels * 8
+    row = lax.broadcasted_iota(jnp.int32, (size, channels), 0) // 8
+    pick = (row == lax.broadcasted_iota(jnp.int32, (size, channels), 1)).astype(F32).astype(BF16)
+    col = lax.broadcasted_iota(jnp.int32, (channels, size), 1) // 8
+    place = (col == lax.broadcasted_iota(jnp.int32, (channels, size), 0)).astype(F32).astype(BF16)
+    left = lax.broadcasted_iota(jnp.int32, (size, size), 0) % 8
+    right = lax.broadcasted_iota(jnp.int32, (size, size), 1) % 8
+
+    def fill(matrix_ref, targets):
+        for part, spots in zip(split(matrix_ref[...]), ((0, 1), (2,))):
+            grown = lax.dot_general(pick, part, (((1,), (1,)), ((), ())), preferred_element_type=F32)
+            grown = dot(grown.astype(BF16), place)
+            for ref, at, rule in targets:
+                value = jnp.where(rule, grown, 0.0).astype(BF16)
+                for spot in spots:
+                    ref[at : at + size, spot * size : (spot + 1) * size] = value
+
+    same = left == right
+    fill(lift_ref, ((lift_wide, 0, same),))
+    fill(middle_ref, ((middle_wide, 0, same),))
+    fill(
+        out_ref,
+        ((proj_wide, 0, same), (final_wide, 0, left // 2 == right), (final_wide, size, left // 2 + 4 == right)),
+    )
+
+
+def prepare(lift_fine, lift_middle, project_out):
+    size = lift_fine.shape[0] * 8
+    shape = jax.ShapeDtypeStruct((size, 3 * size), BF16)
+    return pl.pallas_call(
+        prepare_kernel,
+        out_shape=(shape, shape, shape, jax.ShapeDtypeStruct((2 * size, 3 * size), BF16)),
+        in_specs=[whole()] * 3,
+        out_specs=(whole(),) * 4,
+        name="prepare",
+    )(lift_fine, lift_middle, project_out)
+
+
+def greet(n):
+    me = lax.axis_index("gx")
+    barrier = pltpu.get_barrier_semaphore()
+    for d in range(1, n):
+        pl.semaphore_signal(barrier, 1, device_id={"gx": lax.rem(me + d, n)}, device_id_type=MESH)
+    pl.semaphore_wait(barrier, n - 1)
+
+
+def swap(n, source, target, send_sem, recv_sem, own_sem):
+    me = lax.axis_index("gx")
+    copies = []
+    for d in range(1, n):
+        peer = lax.rem(me + d, n)
+        copy = pltpu.make_async_remote_copy(
+            src_ref=source.at[peer],
+            dst_ref=target.at[me],
+            send_sem=send_sem.at[d],
+            recv_sem=recv_sem.at[d],
+            device_id={"gx": peer},
+            device_id_type=MESH,
+        )
+        copy.start()
+        copies.append(copy)
+    own = pltpu.make_async_copy(source.at[me], target.at[me], own_sem)
+    own.start()
+    for copy in copies:
+        copy.wait()
+    own.wait()
+
+
+def exchange_kernel(n, in_ref, out_ref, send_sem, recv_sem, own_sem):
+    greet(n)
+    swap(n, in_ref, out_ref, send_sem, recv_sem, own_sem)
+
+
+def exchange(values, n, number):
+    return pl.pallas_call(
+        functools.partial(exchange_kernel, n),
+        out_shape=jax.ShapeDtypeStruct(values.shape, F32),
+        in_specs=[whole()],
+        out_specs=whole(),
+        scratch_shapes=[
+            pltpu.SemaphoreType.DMA((n,)),
+            pltpu.SemaphoreType.DMA((n,)),
+            pltpu.SemaphoreType.DMA,
+        ],
+        compiler_params=pltpu.CompilerParams(collective_id=number, has_side_effects=True),
+        name="exchange",
+    )(values)
+
+
+def mix_kernel(
+    n, tx, wire_ref, w_hbm, out_ref, got, w_ref, modal, mixed, back,
+    send_one, recv_one, send_two, recv_two, own_sem, w_sem,
+):
+    modes_x, channels, _, owned = w_ref.shape
+    half = channels // 2
+    fetch = pltpu.make_async_copy(w_hbm, w_ref, w_sem)
+    fetch.start()
+    greet(n)
+    swap(n, wire_ref, got, send_one, recv_one, own_sem.at[0])
+    fetch.wait()
+    lane = lax.broadcasted_iota(jnp.int32, (half, 128), 1)
+    for k in range(modes_x):
+        first = sum(got[a, :channels] * np.float32(tx[k, a, 0]) for a in range(n))
+        second = sum(got[a] * np.float32(tx[k, a, 1]) for a in range(n))
+        extra = jnp.zeros((half, 128), F32)
+        for g in range(3):
+            piece = pltpu.roll(second[g * half : (g + 1) * half], 32 * (g + 1), 1)
+            extra = jnp.where(lane // 32 == g, piece, extra)
+        total = first + jnp.concatenate([second[channels:], extra], 0)
+        modal[k] = total.astype(BF16).astype(F32)
+    mixed[...] = jnp.zeros_like(mixed)
+
+    def mode(k, carry):
+        total = jnp.zeros((channels, owned), F32)
+        for c in range(channels):
+            total += modal[k, c : c + 1, :owned] * w_ref[k, c].astype(F32)
+        mixed[k, :, :owned] = total
+        return carry
+
+    lax.fori_loop(0, modes_x, mode, 0)
+    wide = lax.broadcasted_iota(jnp.int32, (3 * half, 128), 1)
+    for a in range(n):
+        first = sum(mixed[k] * np.float32(tx[k, a, 0]) for k in range(modes_x))
+        second = sum(mixed[k] * np.float32(tx[k, a, 1]) for k in range(modes_x))
+        rolled = jnp.concatenate([pltpu.roll(second[half:], 96 - 32 * g, 1) for g in range(3)], 0)
+        back[a] = jnp.where(wide < 96, jnp.concatenate([first, second[:half]], 0), rolled)
+    swap(n, back, out_ref, send_two, recv_two, own_sem.at[1])
+
+
+def mix_fine(wire, weights, tx, n):
+    turned = jnp.transpose(weights, (1, 2, 3, 0))
+    modes_x, channels = turned.shape[:2]
+    return pl.pallas_call(
+        functools.partial(mix_kernel, n, tx),
+        out_shape=jax.ShapeDtypeStruct(wire.shape, F32),
+        in_specs=[whole(), pl.BlockSpec(memory_space=pl.ANY)],
+        out_specs=whole(),
+        scratch_shapes=[
+            pltpu.VMEM(wire.shape, F32),
+            pltpu.VMEM(turned.shape, BF16),
+            pltpu.VMEM((modes_x, channels, 128), F32),
+            pltpu.VMEM((modes_x, channels, 128), F32),
+            pltpu.VMEM(wire.shape, F32),
+        ]
+        + [pltpu.SemaphoreType.DMA((n,))] * 4
+        + [pltpu.SemaphoreType.DMA((2,)), pltpu.SemaphoreType.DMA],
+        compiler_params=pltpu.CompilerParams(collective_id=0, has_side_effects=True),
+        name="mix_fine",
+    )(wire, turned)
 
 
 def final_kernel(
@@ -353,12 +514,6 @@
     lax.fori_loop(0, half_y // 16, block, 0)
 
 
-def exchange(values, axis_size):
-    rows = values.shape[0] // axis_size
-    flat = values.reshape(axis_size, rows, 128)
-    return lax.all_to_all(flat, "gx", split_axis=0, concat_axis=0, tiled=True)
-
-
 def on_device(features, fine_weights, middle_weights, lift_fine, lift_middle, project_out):
     channels, local_x, cells_y, cells_z = features.shape
     n = lax.axis_size("gx")
@@ -367,7 +522,9 @@
     half_ky, half_kz = KY // 2, KZ // 2
     narrow = 8
     fits = (
-        owned % KZ == 0
+        owned == 3 * KZ
+        and KZ == 32
+        and KY == 3 * n
         and owned_c % narrow == 0
         and local_x == 2
         and cells_z == 128
@@ -380,26 +537,11 @@
         )
     modes_x = fine_weights.shape[1]
     modes_c = middle_weights.shape[1]
-    per_row = 128 // KZ
-    chunks = channels // per_row
-    tx = jnp.asarray(host_table(modes_x, local_x * n), F32).reshape(modes_x, n, local_x)
+    tx = np.asarray(host_table(modes_x, local_x * n), np.float32).reshape(modes_x, n, local_x)
     txc = jnp.asarray(host_table(modes_c, n), F32)
-    lift = blockwise(lift_fine, np.eye(8))
-    proj = blockwise(project_out, np.eye(8))
-    liftm = blockwise(lift_middle, np.eye(8))
-    spread = np.repeat(np.eye(8), 2, axis=0)
-    projm = jnp.concatenate(
-        [blockwise(project_out, spread[8 * b : 8 * b + 8]) for b in range(2)], 0
-    )
-
-    coeffs = forward_fine(features, KY, KZ)
-    got = exchange(coeffs, n)
-    got = got.reshape(n, owned // KZ, local_x, channels, KZ)
-    modal = jnp.einsum("aixcj,kax->ijkc", got, tx, precision=HIGHEST)
-    modal = modal.reshape(owned, modes_x, channels)
-    mixed = mix_modes(modal, fine_weights).reshape(owned // KZ, KZ, modes_x, channels)
-    back = jnp.einsum("ijko,kax->aixoj", mixed, tx, precision=HIGHEST)
-    slab = exchange(back.reshape(-1, 128), n).reshape(-1, 128)
+    lift, liftm, proj, projm = prepare(lift_fine, lift_middle, project_out)
+    wire = forward_fine(features, KY, KZ, n)
+    slab = mix_fine(wire, fine_weights, tx, n)
 
     half_y, half_z = cells_y // 2, cells_z // 2
     pool_y = np.repeat(np.eye(half_y), 2, axis=1) * 0.5
@@ -416,7 +558,7 @@
     zp = np.asarray(zp, jnp.bfloat16)
     zp = jnp.asarray(np.concatenate([zp, zp], 0))
     ty_i = left_three(host_table(KY, cells_y).T)
-    tz_i = right_three(np.tile(host_table(KZ, cells_z), (per_row, 1)))
+    tz_i = right_three(np.tile(host_table(KZ, cells_z), (4, 1)))
     base, pooled, coarse = pl.pallas_call(
         middle_kernel,
         out_shape=(
@@ -429,16 +571,19 @@
         scratch_shapes=[
             pltpu.VMEM(features.shape, F32),
             pltpu.VMEM((channels, cells_y, cells_z), F32),
+            pltpu.VMEM((KY * local_x * channels, cells_z), F32),
         ],
         name="middle",
     )(slab, features, ty_i, tz_i, lift, proj, yc, zc, zp)
 
-    got = exchange(coarse, n).reshape(n, owned_c // narrow, chunks_c, per_c, narrow)
-    modal = jnp.einsum("aqhlj,ka->qjkhl", got, txc, precision=HIGHEST)
+    count = owned_c // narrow
+    got = exchange(coarse.reshape(n, -1, 128), n, 1).reshape(n, -1)
+    modal = jnp.einsum("ar,ka->kr", got, txc, precision=HIGHEST)
+    modal = modal.reshape(modes_c, count, channels, narrow).transpose(1, 3, 0, 2)
     mixed = mix_modes(modal.reshape(owned_c, modes_c, channels), middle_weights)
-    mixed = mixed.reshape(owned_c // narrow, narrow, modes_c, chunks_c, per_c)
-    back = jnp.einsum("qjkhl,ka->aqhlj", mixed, txc, precision=HIGHEST)
-    slab = exchange(back.reshape(-1, 128), n).reshape(-1, 128)
+    mixed = mixed.reshape(count, narrow, modes_c, channels).transpose(2, 0, 3, 1)
+    back = jnp.einsum("kr,ka->ar", mixed.reshape(modes_c, -1), txc, precision=HIGHEST)
+    slab = exchange(back.reshape(n, -1, 128), n, 2).reshape(-1, 128)
 
     tyc_i = left_three(ty_c.T)
     grown = np.repeat(tz_c, 2, axis=1).reshape(parts, 1, narrow, cells_z)

time: 226 us -> 121 us (0.54)
  local copies, waits for them, and re-layouts: 96.6 us -> 4.38 us
  Pallas kernels: 53.6 us -> 114 us
  starting transfers between devices: 25.4 us -> 0 us
  other arithmetic: 21.6 us -> 0 us
  matrix products: 19.4 us -> 1.79 us
  waiting for transfers between devices: 6.91 us -> 0 us
    mul x10 -> x0, local copies, waits for them, and re-layouts: 65.6 us -> none  [blockwise(): grown = part.T[:, None, :, None] * jnp.asarray(left, BF16)[None, :, None, :]]
    pallas_call x1 -> x5, Pallas kernels: 11.9 us -> 70.9 us  [the longest x1 32.1 us: mix_fine(): pl.pallas_call(functools.partial(mix_kernel, n, tx), out_shape=jax.ShapeD...]
    all_to_all x4 -> x0, starting transfers between devices: 25.4 us -> none  [exchange(): return lax.all_to_all(flat, 'gx', split_axis=0, concat_axis=0, tiled=True)]
    unnamed x17 -> x4, local copies, waits for them, and re-layouts: 16.7 us -> 0.01 us
    mul x1 -> x0, other arithmetic: 16.6 us -> none  [blockwise(): grown = part.T[:, None, :, None] * jnp.asarray(left, BF16)[None, :, None, :]]
    dot_general x4 -> x2, matrix products: 13.9 us -> 1.36 us  [the longest x1 1.09 us: on_device(): modal = jnp.einsum('ar,ka->kr', got, txc, precision=HIGHEST)]
    all_to_all x4 -> x0, waiting for transfers between devices: 6.91 us -> none  [exchange(): return lax.all_to_all(flat, 'gx', split_axis=0, concat_axis=0, tiled=True)]
    transpose x8 -> x1, local copies, waits for them, and re-layouts: 5.67 us -> 0.14 us  [on_device(): mixed.reshape(count, narrow, modes_c, channels).transpose(2, 0, 3, 1)]
  transfers between devices with their start and end apart: 4 -> 0, of which waited for: 1 -> 0; matrix products, arithmetic and copies ran while one was open for 48% -> 0% of each run, Pallas kernels for 0% -> 0%
where the time goes in v1:
time: 121 us; the launch traced here: 120 us
  Pallas kernels  114 us (94%)
  local copies, waits for them, and re-layouts  4.38 us (4%)
  matrix products  1.79 us (1%)
    pallas_call x1, Pallas kernels, mix_fine(): pl.pallas_call(functools.partial(mix_kernel, n, tx), out_shape=jax.ShapeD...  32.1 us
    pallas_call x1, Pallas kernels, on_device(): pl.pallas_call(middle_kernel, out_shape=(jax.ShapeDtypeStruct(features.sh...  31.5 us
    pallas_call x2, Pallas kernels, exchange(): pl.pallas_call(functools.partial(exchange_kernel, n), out_shape=jax.Shape...  22.3 us
    pallas_call x1, Pallas kernels, forward_fine(): pl.pallas_call(forward_kernel, grid=(channels // block,), out_shape=jax.S...  12.7 us
    pallas_call x1, Pallas kernels, on_device(): pl.pallas_call(final_kernel, out_shape=jax.ShapeDtypeStruct(features.shap...  11.7 us
    pallas_call x1, Pallas kernels, prepare(): pl.pallas_call(prepare_kernel, out_shape=(shape, shape, shape, jax.ShapeD...  3.81 us

profile of v1, /device:TPU:0, one launch (start us, length us, event | category | flops | bytes accessed | tf_op | source)
XLA Modules:
  0.0 120.3 jit_solution(4020336360624859703)
XLA Ops:
  0.0 0.0 copy-start
  0.0 12.7 %forward_fine.1.wire_ref = f32[16,72,128]{2,1,0:T(8,128)} custom-call(f32[48,2,96,128]{3,2,1,0:T(8,128)} %f_ref.3, bf16[96,192]{1,0:T(8,128)(2,1)} %constant.21.clone.ty_ref, bf16[384,128]{1,0:T(8,128)(2,1)} %constant.22.clone.tz_ref), custom_call_target="tpu_custom_call" | custom-call | tf_op jit(solution)/shard_map/forward_fine/pallas_call | solution.py:215
  12.7 32.1 %mix_fine.1.slab_ref = f32[16,72,128]{2,1,0:T(8,128)} custom-call(f32[16,72,128]{2,1,0:T(8,128)} %forward_fine.1.wire_ref, bf16[8,48,48,96]{3,2,1,0:T(8,128)(2,1)} %bitcast.24), custom_call_target="tpu_custom_call" | custom-call | tf_op jit(solution)/shard_map/mix_fine/pallas_call | solution.py:454
  44.8 3.8 %prepare.1 = (bf16[384,1152]{1,0:T(8,128)(2,1)}, bf16[384,1152]{1,0:T(8,128)(2,1)}, bf16[384,1152]{1,0:T(8,128)(2,1)}, bf16[768,1152]{1,0:T(8,128)(2,1)}) custom-call(f32[48,48]{1,0:T(8,128)} %lift_ref.1, f32[48,48]{1,0:T(8,128)} %middle_ref.1, f32[48,48]{1,0:T(8,128)} %out_ref.1), custom_call_target="tpu_custom_call" | custom-call | tf_op jit(solution)/shard_map/prepare/pallas_call | solution.py:351
  48.6 0.0 copy-start.1
  48.6 31.5 %middle.1 = (f32[48,2,96,128]{3,2,1,0:T(8,128)}, f32[48,48,128]{2,1,0:T(8,128)}, f32[144,128]{1,0:T(8,128)}) custom-call(f32[16,72,128]{2,1,0:T(8,128)} %mix_fine.1.slab_ref, f32[48,2,96,128]{3,2,1,0:T(8,128)} %f_ref.3, bf16[96,144]{1,0:T(8,128)(2,1)} %constant.26.clone.ty_ref, bf16[384,128]{1,0:T(8,128)(2,1)} %constant.27.clone.tz_ref, ...), custom_call_target="tpu_custom_call" | custom-call | tf_op jit(solution)/shard_map/middle/pallas_call | solution.py:562
  80.0 1.5 %reshape.22.in_ref = f32[16,9,128]{2,1,0:T(8,128)} reshape(f32[144,128]{1,0:T(8,128)} %get-tuple-element.14) | data formatting | bytes 147456 | tf_op jit(solution)/shard_map/reshape | solution.py:580
  81.6 13.8 %exchange.2 = f32[16,9,128]{2,1,0:T(8,128)} custom-call(f32[16,9,128]{2,1,0:T(8,128)} %reshape.22.in_ref), custom_call_target="tpu_custom_call" | custom-call | tf_op jit(solution)/shard_map/exchange/pallas_call | solution.py:396
  95.4 0.0 copy-done.1
  95.4 1.1 fusion
  96.5 0.2 convert_element_type.17
  96.7 0.1 copy.18
  96.8 0.0 copy-done
  96.8 0.4 fusion.3
  97.3 0.1 copy.19
  97.4 0.2 reshape.25
  97.6 0.3 fusion.5
  97.9 0.7 reshape.26.in_ref
  98.6 8.5 %exchange.3 = f32[16,9,128]{2,1,0:T(8,128)} custom-call(f32[16,9,128]{2,1,0:T(8,128)} %reshape.26.in_ref), custom_call_target="tpu_custom_call" | custom-call | tf_op jit(solution)/shard_map/exchange/pallas_call | solution.py:396
  107.0 1.5 %reshape.27.slab_ref = f32[144,128]{1,0:T(8,128)} reshape(f32[16,9,128]{2,1,0:T(8,128)} %exchange.3) | data formatting | bytes 147456 | tf_op jit(solution)/shard_map/reshape | solution.py:586
  108.6 11.7 %final.1 = f32[48,2,96,128]{3,2,1,0:T(8,128)} custom-call(f32[144,128]{1,0:T(8,128)} %reshape.27.slab_ref, f32[48,48,128]{2,1,0:T(8,128)} %get-tuple-element.15.pooled_ref, f32[48,2,96,128]{3,2,1,0:T(8,128)} %get-tuple-element.16.base_ref, bf16[48,72]{1,0:T(8,128)(2,1)} %constant.28.clone.ty_ref, bf16[768,128]{1,0:T(8,128)(2,1)} %constant.29.clone.tz_ref, ...), custom_call_target="tpu_custom_call" | custom-call | tf_op jit(solution)/shard_map/final/pallas_call | solution.py:591
  (1 shorter events, 0.0 us)
Async XLA Ops:
  0.0 96.8 %copy-start = (bf16[24,4,48,48]{3,2,1,0:T(8,128)(2,1)S(1)}, bf16[24,4,48,48]{3,2,1,0:T(8,128)(2,1)}, u32[]{:S(2)}) copy-start(bf16[24,4,48,48]{3,2,1,0:T(8,128)(2,1)} %param.18) | copy-start | bytes 1327108
  48.6 46.9 %copy-start.1 = (f32[4,16]{1,0:T(4,128)S(1)}, f32[4,16]{1,0:T(4,128)}, u32[]{:S(2)}) copy-start(f32[4,16]{1,0:T(4,128)} %constant.20.clone) | copy-start | bytes 772

commit v2 on v1

--- a/solution.py
+++ b/solution.py
@@ -228,8 +228,8 @@
 
 
 def middle_kernel(
-    slab_ref, f_ref, ty_ref, tz_ref, lift_ref, proj_ref, yc_ref, zc_ref, zp_ref,
-    base_ref, pooled_ref, coarse_ref, spec_ref, sum_ref, grown_ref,
+    slab_ref, f_ref, ty_ref, tz_ref, yc_ref, zc_ref, zp_ref,
+    level_ref, pooled_ref, coarse_ref, spec_ref, sum_ref, grown_ref,
 ):
     channels, local_x, cells_y, cells_z = f_ref.shape
     modes_y = ty_ref.shape[1] // 3
@@ -262,22 +262,14 @@
 
     lax.fori_loop(0, channels, inverse_y, 0, unroll=4)
 
-    def block(b, carry):
-        at = pl.ds(pl.multiple_of(b * 8, 8), 8)
-        values = jnp.concatenate(
-            [f_ref[:, x, at, :].reshape(channels * 8, cells_z) for x in range(local_x)], 1
-        )
-        spectral = jnp.concatenate(
-            [spec_ref[:, x, at, :].reshape(channels * 8, cells_z) for x in range(local_x)], 1
-        )
-        level = gelu(dot_left3(lift_ref[...], values) + spectral)
-        base = values + dot_left3(proj_ref[...], level)
+    def block(o, carry):
+        level = [gelu(f_ref[o, x] + spec_ref[o, x]) for x in range(local_x)]
         for x in range(local_x):
-            base_ref[:, x, at, :] = base[:, x * cells_z : (x + 1) * cells_z].reshape(channels, 8, cells_z)
-        sum_ref[:, at, :] = (level[:, :cells_z] + level[:, cells_z:]).reshape(channels, 8, cells_z)
+            level_ref[o, x] = level[x]
+        sum_ref[o] = level[0] + level[1]
         return carry
 
-    lax.fori_loop(0, cells_y // 8, block, 0)
+    lax.fori_loop(0, channels, block, 0)
 
     half_y = cells_y // 2
     modes_c = yc_ref.shape[0] // 2 - half_y
@@ -317,8 +309,8 @@
     lax.fori_loop(0, coarse_chunks, coarse, 0)
 
 
-def prepare_kernel(lift_ref, middle_ref, out_ref, lift_wide, middle_wide, proj_wide, final_wide):
-    channels = lift_ref.shape[0]
+def widen(matrix_ref, targets):
+    channels = matrix_ref.shape[0]
     size = channels * 8
     row = lax.broadcasted_iota(jnp.int32, (size, channels), 0) // 8
     pick = (row == lax.broadcasted_iota(jnp.int32, (size, channels), 1)).astype(F32).astype(BF16)
@@ -326,35 +318,28 @@
     place = (col == lax.broadcasted_iota(jnp.int32, (channels, size), 0)).astype(F32).astype(BF16)
     left = lax.broadcasted_iota(jnp.int32, (size, size), 0) % 8
     right = lax.broadcasted_iota(jnp.int32, (size, size), 1) % 8
-
-    def fill(matrix_ref, targets):
-        for part, spots in zip(split(matrix_ref[...]), ((0, 1), (2,))):
-            grown = lax.dot_general(pick, part, (((1,), (1,)), ((), ())), preferred_element_type=F32)
-            grown = dot(grown.astype(BF16), place)
-            for ref, at, rule in targets:
-                value = jnp.where(rule, grown, 0.0).astype(BF16)
-                for spot in spots:
-                    ref[at : at + size, spot * size : (spot + 1) * size] = value
-
-    same = left == right
-    fill(lift_ref, ((lift_wide, 0, same),))
-    fill(middle_ref, ((middle_wide, 0, same),))
-    fill(
-        out_ref,
-        ((proj_wide, 0, same), (final_wide, 0, left // 2 == right), (final_wide, size, left // 2 + 4 == right)),
-    )
-
-
-def prepare(lift_fine, lift_middle, project_out):
-    size = lift_fine.shape[0] * 8
-    shape = jax.ShapeDtypeStruct((size, 3 * size), BF16)
-    return pl.pallas_call(
-        prepare_kernel,
-        out_shape=(shape, shape, shape, jax.ShapeDtypeStruct((2 * size, 3 * size), BF16)),
-        in_specs=[whole()] * 3,
-        out_specs=(whole(),) * 4,
-        name="prepare",
-    )(lift_fine, lift_middle, project_out)
+    for part, spots in zip(split(matrix_ref[...]), ((0, 1), (2,))):
+        grown = lax.dot_general(pick, part, (((1,), (1,)), ((), ())), preferred_element_type=F32)
+        grown = dot(grown.astype(BF16), place)
+        for ref, at, rule in targets:
+            value = jnp.where(rule(left, right), grown, 0.0).astype(BF16)
+            for spot in spots:
+                ref[at : at + size, spot * size : (spot + 1) * size] = value
+
+
+def same(left, right):
+    return left == right
+
+
+def load_block(ref, at):
+    channels, local_x, _, cells_z = ref.shape
+    return jnp.concatenate([ref[:, x, at, :].reshape(channels * 8, cells_z) for x in range(local_x)], 1)
+
+
+def store_block(ref, at, value):
+    channels, local_x, _, cells_z = ref.shape
+    for x in range(local_x):
+        ref[:, x, at, :] = value[:, x * cells_z : (x + 1) * cells_z].reshape(channels, 8, cells_z)
 
 
 def greet(n):
@@ -365,7 +350,7 @@
     pl.semaphore_wait(barrier, n - 1)
 
 
-def swap(n, source, target, send_sem, recv_sem, own_sem):
+def swap(n, source, target, send_sem, recv_sem, own_sem, work):
     me = lax.axis_index("gx")
     copies = []
     for d in range(1, n):
@@ -382,34 +367,80 @@
         copies.append(copy)
     own = pltpu.make_async_copy(source.at[me], target.at[me], own_sem)
     own.start()
+    work()
     for copy in copies:
         copy.wait()
     own.wait()
 
 
-def exchange_kernel(n, in_ref, out_ref, send_sem, recv_sem, own_sem):
+def coarse_out_kernel(
+    n, tx, in_ref, f_ref, level_ref, wide_ref, out_ref, base_ref, stage, got, send_sem, recv_sem, own_sem
+):
+    rows = stage.shape[1]
+    for a in range(n):
+        stage[a] = in_ref[a * rows : (a + 1) * rows]
     greet(n)
-    swap(n, in_ref, out_ref, send_sem, recv_sem, own_sem)
-
-
-def exchange(values, n, number):
+
+    def work():
+        def block(b, carry):
+            at = pl.ds(pl.multiple_of(b * 8, 8), 8)
+            done = dot_left3(wide_ref[...], load_block(level_ref, at))
+            store_block(base_ref, at, load_block(f_ref, at) + done)
+            return carry
+
+        lax.fori_loop(0, f_ref.shape[2] // 8, block, 0)
+
+    swap(n, stage, got, send_sem, recv_sem, own_sem, work)
+    for k in range(out_ref.shape[0]):
+        out_ref[k] = sum(got[a] * np.float32(tx[k, a]) for a in range(n))
+
+
+def coarse_back_kernel(
+    n, tx, in_ref, pooled_ref, wide_ref, out_ref, lifted_ref, stage, got, send_sem, recv_sem, own_sem
+):
+    rows = stage.shape[1]
+    for a in range(n):
+        stage[a] = sum(in_ref[k] * np.float32(tx[k, a]) for k in range(in_ref.shape[0]))
+    greet(n)
+    channels, half_y, _ = pooled_ref.shape
+
+    def work():
+        def block(g, carry):
+            at = [pl.ds(pl.multiple_of(g * 16 + 8 * k, 8), 8) for k in range(2)]
+            pooled = jnp.concatenate([pooled_ref[:, a, :].reshape(channels * 8, 128) for a in at], 1)
+            done = dot_left3(wide_ref[...], pooled)
+            for k in range(2):
+                lifted_ref[:, at[k], :] = done[:, k * 128 : (k + 1) * 128].reshape(channels, 8, 128)
+            return carry
+
+        lax.fori_loop(0, half_y // 16, block, 0)
+
+    swap(n, stage, got, send_sem, recv_sem, own_sem, work)
+    for a in range(n):
+        out_ref[a * rows : (a + 1) * rows] = got[a]
+
+
+def coarse_call(kernel, n, tx, rows, number, shapes, *values):
     return pl.pallas_call(
-        functools.partial(exchange_kernel, n),
-        out_shape=jax.ShapeDtypeStruct(values.shape, F32),
-        in_specs=[whole()],
-        out_specs=whole(),
+        functools.partial(kernel, n, tx),
+        out_shape=tuple(jax.ShapeDtypeStruct(shape, F32) for shape in shapes),
+        in_specs=[whole()] * len(values),
+        out_specs=(whole(),) * len(shapes),
         scratch_shapes=[
+            pltpu.VMEM((n, rows, 128), F32),
+            pltpu.VMEM((n, rows, 128), F32),
             pltpu.SemaphoreType.DMA((n,)),
             pltpu.SemaphoreType.DMA((n,)),
             pltpu.SemaphoreType.DMA,
         ],
         compiler_params=pltpu.CompilerParams(collective_id=number, has_side_effects=True),
-        name="exchange",
-    )(values)
+        name=kernel.__name__,
+    )(*values)
 
 
 def mix_kernel(
-    n, tx, wire_ref, w_hbm, out_ref, got, w_ref, modal, mixed, back,
+    n, tx, wire_ref, w_hbm, f_ref, lift_ref, middle_ref, project_ref,
+    out_ref, lifted_ref, middle_wide, proj_wide, final_wide, lift_wide, got, w_ref, modal, mixed, back,
     send_one, recv_one, send_two, recv_two, own_sem, w_sem,
 ):
     modes_x, channels, _, owned = w_ref.shape
@@ -417,7 +448,18 @@
     fetch = pltpu.make_async_copy(w_hbm, w_ref, w_sem)
     fetch.start()
     greet(n)
-    swap(n, wire_ref, got, send_one, recv_one, own_sem.at[0])
+
+    def lift():
+        widen(lift_ref, ((lift_wide, 0, same),))
+
+        def block(b, carry):
+            at = pl.ds(pl.multiple_of(b * 8, 8), 8)
+            store_block(lifted_ref, at, dot_left3(lift_wide[...], load_block(f_ref, at)))
+            return carry
+
+        lax.fori_loop(0, f_ref.shape[2] // 8, block, 0)
+
+    swap(n, wire_ref, got, send_one, recv_one, own_sem.at[0], lift)
     fetch.wait()
     lane = lax.broadcasted_iota(jnp.int32, (half, 128), 1)
     for k in range(modes_x):
@@ -445,18 +487,40 @@
         second = sum(mixed[k] * np.float32(tx[k, a, 1]) for k in range(modes_x))
         rolled = jnp.concatenate([pltpu.roll(second[half:], 96 - 32 * g, 1) for g in range(3)], 0)
         back[a] = jnp.where(wide < 96, jnp.concatenate([first, second[:half]], 0), rolled)
-    swap(n, back, out_ref, send_two, recv_two, own_sem.at[1])
-
-
-def mix_fine(wire, weights, tx, n):
+
+    def matrices():
+        size = channels * 8
+        widen(middle_ref, ((middle_wide, 0, same),))
+        widen(
+            project_ref,
+            (
+                (proj_wide, 0, same),
+                (final_wide, 0, lambda left, right: left // 2 == right),
+                (final_wide, size, lambda left, right: left // 2 + 4 == right),
+            ),
+        )
+
+    swap(n, back, out_ref, send_two, recv_two, own_sem.at[1], matrices)
+
+
+def mix_fine(wire, weights, features, matrices, tx, n):
     turned = jnp.transpose(weights, (1, 2, 3, 0))
     modes_x, channels = turned.shape[:2]
+    size = channels * 8
+    wide = jax.ShapeDtypeStruct((size, 3 * size), BF16)
     return pl.pallas_call(
         functools.partial(mix_kernel, n, tx),
-        out_shape=jax.ShapeDtypeStruct(wire.shape, F32),
-        in_specs=[whole(), pl.BlockSpec(memory_space=pl.ANY)],
-        out_specs=whole(),
+        out_shape=(
+            jax.ShapeDtypeStruct(wire.shape, F32),
+            jax.ShapeDtypeStruct(features.shape, F32),
+            wide,
+            wide,
+            jax.ShapeDtypeStruct((2 * size, 3 * size), BF16),
+        ),
+        in_specs=[whole(), pl.BlockSpec(memory_space=pl.ANY)] + [whole()] * 4,
+        out_specs=(whole(),) * 5,
         scratch_shapes=[
+            pltpu.VMEM(wide.shape, BF16),
             pltpu.VMEM(wire.shape, F32),
             pltpu.VMEM(turned.shape, BF16),
             pltpu.VMEM((modes_x, channels, 128), F32),
@@ -467,11 +531,11 @@
         + [pltpu.SemaphoreType.DMA((2,)), pltpu.SemaphoreType.DMA],
         compiler_params=pltpu.CompilerParams(collective_id=0, has_side_effects=True),
         name="mix_fine",
-    )(wire, turned)
+    )(wire, turned, features, *matrices)
 
 
 def final_kernel(
-    slab_ref, pooled_ref, base_ref, ty_ref, tz_ref, lift_ref, proj_ref, out_ref, spec_ref
+    slab_ref, pooled_ref, base_ref, ty_ref, tz_ref, proj_ref, out_ref, spec_ref
 ):
     channels, half_y, _ = pooled_ref.shape
     local_x = base_ref.shape[1]
@@ -500,7 +564,7 @@
         at = [pl.ds(pl.multiple_of(g * 16 + 8 * k, 8), 8) for k in range(2)]
         pooled = jnp.concatenate([pooled_ref[:, a, :].reshape(channels * 8, 128) for a in at], 1)
         spectral = jnp.concatenate([spec_ref[:, a, :].reshape(channels * 8, 128) for a in at], 1)
-        level = gelu(dot_left3(lift_ref[...], pooled) + spectral)
+        level = gelu(pooled + spectral)
         added = dot_left3(proj_ref[...], level)
         for k in range(2):
             for b in range(2):
@@ -538,10 +602,11 @@
     modes_x = fine_weights.shape[1]
     modes_c = middle_weights.shape[1]
     tx = np.asarray(host_table(modes_x, local_x * n), np.float32).reshape(modes_x, n, local_x)
-    txc = jnp.asarray(host_table(modes_c, n), F32)
-    lift, liftm, proj, projm = prepare(lift_fine, lift_middle, project_out)
+    txc = np.asarray(host_table(modes_c, n), np.float32)
     wire = forward_fine(features, KY, KZ, n)
-    slab = mix_fine(wire, fine_weights, tx, n)
+    slab, lifted, liftm, proj, projm = mix_fine(
+        wire, fine_weights, features, (lift_fine, lift_middle, project_out), tx, n
+    )
 
     half_y, half_z = cells_y // 2, cells_z // 2
     pool_y = np.repeat(np.eye(half_y), 2, axis=1) * 0.5
@@ -559,14 +624,14 @@
     zp = jnp.asarray(np.concatenate([zp, zp], 0))
     ty_i = left_three(host_table(KY, cells_y).T)
     tz_i = right_three(np.tile(host_table(KZ, cells_z), (4, 1)))
-    base, pooled, coarse = pl.pallas_call(
+    level, pooled, coarse = pl.pallas_call(
         middle_kernel,
         out_shape=(
             jax.ShapeDtypeStruct(features.shape, F32),
             jax.ShapeDtypeStruct((channels, half_y, 128), F32),
             jax.ShapeDtypeStruct((half_ky * parts * chunks_c, 128), F32),
         ),
-        in_specs=[whole()] * 9,
+        in_specs=[whole()] * 7,
         out_specs=(whole(), whole(), whole()),
         scratch_shapes=[
             pltpu.VMEM(features.shape, F32),
@@ -574,16 +639,21 @@
             pltpu.VMEM((KY * local_x * channels, cells_z), F32),
         ],
         name="middle",
-    )(slab, features, ty_i, tz_i, lift, proj, yc, zc, zp)
+    )(slab, lifted, ty_i, tz_i, yc, zc, zp)
 
     count = owned_c // narrow
-    got = exchange(coarse.reshape(n, -1, 128), n, 1).reshape(n, -1)
-    modal = jnp.einsum("ar,ka->kr", got, txc, precision=HIGHEST)
+    rows = count * chunks_c
+    modal, base = coarse_call(
+        coarse_out_kernel, n, txc, rows, 1, ((modes_c, rows, 128), features.shape),
+        coarse, features, level, proj,
+    )
     modal = modal.reshape(modes_c, count, channels, narrow).transpose(1, 3, 0, 2)
     mixed = mix_modes(modal.reshape(owned_c, modes_c, channels), middle_weights)
     mixed = mixed.reshape(count, narrow, modes_c, channels).transpose(2, 0, 3, 1)
-    back = jnp.einsum("kr,ka->ar", mixed.reshape(modes_c, -1), txc, precision=HIGHEST)
-    slab = exchange(back.reshape(n, -1, 128), n, 2).reshape(-1, 128)
+    slab, lifted = coarse_call(
+        coarse_back_kernel, n, txc, rows, 2, ((n * rows, 128), pooled.shape),
+        mixed.reshape(modes_c, rows, 128), pooled, liftm,
+    )
 
     tyc_i = left_three(ty_c.T)
     grown = np.repeat(tz_c, 2, axis=1).reshape(parts, 1, narrow, cells_z)
@@ -591,11 +661,11 @@
     return pl.pallas_call(
         final_kernel,
         out_shape=jax.ShapeDtypeStruct(features.shape, F32),
-        in_specs=[whole()] * 7,
+        in_specs=[whole()] * 6,
         out_specs=whole(),
         scratch_shapes=[pltpu.VMEM((channels, half_y, 128), F32)],
         name="final",
-    )(slab, pooled, base, tyc_i, tzc_i, liftm, projm)
+    )(slab, lifted, base, tyc_i, tzc_i, projm)
 
 
 def solution(mesh):

time: 121 us -> 108 us (0.89)
  Pallas kernels: 114 us -> 106 us
  local copies, waits for them, and re-layouts: 4.38 us -> 1.23 us
  matrix products: 1.79 us -> 0.43 us
    pallas_call x1, Pallas kernels: 31.5 us -> 17.2 us  [on_device(): pl.pallas_call(middle_kernel, out_shape=(jax.ShapeDtypeStruct(features.sh...]
    pallas_call x4 -> x3, Pallas kernels: 58.2 us -> 66.8 us  [the longest x1 36.1 us: mix_fine(): pl.pallas_call(functools.partial(mix_kernel, n, tx), out_shape=(jax.Shape...]
    reshape x4 -> x1, local copies, waits for them, and re-layouts: 3.94 us -> 0.79 us  [on_device(): mixed.reshape(modes_c, rows, 128)]
    pallas_call x1, Pallas kernels: 11.7 us -> 9 us  [on_device(): pl.pallas_call(final_kernel, out_shape=jax.ShapeDtypeStruct(features.shap...]
    dot_general x2 -> x0, matrix products: 1.36 us -> none  [the longest x1 1.09 us: on_device(): modal = jnp.einsum('ar,ka->kr', got, txc, precision=HIGHEST)]
where the time goes in v2:
time: 108 us
  Pallas kernels  106 us (98%)
  local copies, waits for them, and re-layouts  1.23 us (1%)
    pallas_call x1, Pallas kernels, mix_fine(): pl.pallas_call(functools.partial(mix_kernel, n, tx), out_shape=(jax.Shape...  36.1 us
    pallas_call x2, Pallas kernels, coarse_call(): pl.pallas_call(functools.partial(kernel, n, tx), out_shape=tuple((jax.Sha...  30.7 us
    pallas_call x1, Pallas kernels, on_device(): pl.pallas_call(middle_kernel, out_shape=(jax.ShapeDtypeStruct(features.sh...  17.2 us
    pallas_call x1, Pallas kernels, forward_fine(): pl.pallas_call(forward_kernel, grid=(channels // block,), out_shape=jax.S...  12.7 us
    pallas_call x1, Pallas kernels, on_device(): pl.pallas_call(final_kernel, out_shape=jax.ShapeDtypeStruct(features.shap...  9 us

profile of v2, /device:TPU:0, one launch (start us, length us, event | category | flops | bytes accessed | tf_op | source)
XLA Modules:
  0.0 108.1 jit_solution(6988649397148354433)
XLA Ops:
  0.0 0.0 copy-start
  0.0 12.7 %forward_fine.1.wire_ref = f32[16,72,128]{2,1,0:T(8,128)} custom-call(f32[48,2,96,128]{3,2,1,0:T(8,128)} %f_ref.5, bf16[96,192]{1,0:T(8,128)(2,1)} %constant.18.clone.ty_ref, bf16[384,128]{1,0:T(8,128)(2,1)} %constant.19.clone.tz_ref), custom_call_target="tpu_custom_call" | custom-call | tf_op jit(solution)/shard_map/forward_fine/pallas_call | solution.py:215
  12.7 36.1 %mix_fine.1 = (f32[16,72,128]{2,1,0:T(8,128)}, f32[48,2,96,128]{3,2,1,0:T(8,128)}, bf16[384,1152]{1,0:T(8,128)(2,1)}, bf16[384,1152]{1,0:T(8,128)(2,1)}, bf16[768,1152]{1,0:T(8,128)(2,1)}) custom-call(f32[16,72,128]{2,1,0:T(8,128)} %forward_fine.1.wire_ref, bf16[8,48,48,96]{3,2,1,0:T(8,128)(2,1)} %bitcast.15, f32[48,2,96,128]{3,2,1,0:T(8,128)} %f_ref.5, ...), custom_call_target="tpu_custom_call" | custom-call | tf_op jit(solution)/shard_map/mix_fine/pallas_call | solution.py:511
  48.8 17.2 %middle.1 = (f32[48,2,96,128]{3,2,1,0:T(8,128)}, f32[48,48,128]{2,1,0:T(8,128)}, f32[144,128]{1,0:T(8,128)}) custom-call(f32[16,72,128]{2,1,0:T(8,128)} %get-tuple-element.17.slab_ref, f32[48,2,96,128]{3,2,1,0:T(8,128)} %get-tuple-element.18.f_ref, bf16[96,144]{1,0:T(8,128)(2,1)} %constant.23.clone.ty_ref, bf16[384,128]{1,0:T(8,128)(2,1)} %constant.24.clone.tz_ref, ...), custom_call_target="tpu_custom_call" | custom-call | tf_op jit(solution)/shard_map/middle/pallas_call | solution.py:627
  66.0 21.2 %coarse_out_kernel.1 = (f32[4,9,128]{2,1,0:T(8,128)}, f32[48,2,96,128]{3,2,1,0:T(8,128)}) custom-call(f32[144,128]{1,0:T(8,128)} %get-tuple-element.19.in_ref, f32[48,2,96,128]{3,2,1,0:T(8,128)} %f_ref.5, f32[48,2,96,128]{3,2,1,0:T(8,128)} %get-tuple-element.20.level_ref, bf16[384,1152]{1,0:T(8,128)(2,1)} %get-tuple-element.21.wide_ref), custom_call_target="tpu_custom_call" | custom-call | tf_op jit(solution)/shard_map/coarse_out_kernel/pallas_call | solution.py:424
  87.2 0.8 convert_element_type.12
  87.9 0.2 convert_element_type.13
  88.1 0.1 copy.16
  88.2 0.0 copy-done
  88.2 0.4 fusion
  88.7 0.1 copy.17
  88.8 0.8 reshape.11.in_ref
  89.6 9.5 %coarse_back_kernel.1 = (f32[144,128]{1,0:T(8,128)}, f32[48,48,128]{2,1,0:T(8,128)}) custom-call(f32[4,9,128]{2,1,0:T(8,128)} %reshape.11.in_ref, f32[48,48,128]{2,1,0:T(8,128)} %get-tuple-element.23.pooled_ref, bf16[384,1152]{1,0:T(8,128)(2,1)} %get-tuple-element.24.wide_ref), custom_call_target="tpu_custom_call" | custom-call | tf_op jit(solution)/shard_map/coarse_back_kernel/pallas_call | solution.py:424
  99.1 9.0 %final.1 = f32[48,2,96,128]{3,2,1,0:T(8,128)} custom-call(f32[144,128]{1,0:T(8,128)} %get-tuple-element.25.slab_ref, f32[48,48,128]{2,1,0:T(8,128)} %get-tuple-element.26.pooled_ref, f32[48,2,96,128]{3,2,1,0:T(8,128)} %get-tuple-element.27.base_ref, bf16[48,72]{1,0:T(8,128)(2,1)} %constant.25.clone.ty_ref, bf16[768,128]{1,0:T(8,128)(2,1)} %constant.26.clone.tz_ref, ...), custom_call_target="tpu_custom_call" | custom-call | tf_op jit(solution)/shard_map/final/pallas_call | solution.py:661
  (1 shorter events, 0.0 us)
Async XLA Ops:
  0.0 88.2 %copy-start = (bf16[24,4,48,48]{3,2,1,0:T(8,128)(2,1)S(1)}, bf16[24,4,48,48]{3,2,1,0:T(8,128)(2,1)}, u32[]{:S(2)}) copy-start(bf16[24,4,48,48]{3,2,1,0:T(8,128)(2,1)} %param.17) | copy-start | bytes 1327108

commit v3 on v2

--- a/solution.py
+++ b/solution.py
@@ -165,6 +165,10 @@
 
 def gelu(t):
     return 0.5 * t * (1.0 + lax.erf(t * np.float32(np.sqrt(0.5))))
+
+
+def far():
+    return pl.BlockSpec(memory_space=pl.ANY)
 
 
 def whole():
@@ -228,9 +232,12 @@
 
 
 def middle_kernel(
-    slab_ref, f_ref, ty_ref, tz_ref, yc_ref, zc_ref, zp_ref,
-    level_ref, pooled_ref, coarse_ref, spec_ref, sum_ref, grown_ref,
+    slab_ref, f_hbm, ty_ref, tz_ref, yc_ref, zc_ref, zp_ref,
+    level_hbm, pooled_ref, coarse_ref, spec_ref, sum_ref, grown_ref, f_ref, move_sem,
 ):
+    load = pltpu.make_async_copy(f_hbm, f_ref, move_sem.at[0])
+    load.start()
+    save = pltpu.make_async_copy(f_ref, level_hbm, move_sem.at[1])
     channels, local_x, cells_y, cells_z = f_ref.shape
     modes_y = ty_ref.shape[1] // 3
     n = slab_ref.shape[0]
@@ -262,14 +269,17 @@
 
     lax.fori_loop(0, channels, inverse_y, 0, unroll=4)
 
+    load.wait()
+
     def block(o, carry):
         level = [gelu(f_ref[o, x] + spec_ref[o, x]) for x in range(local_x)]
         for x in range(local_x):
-            level_ref[o, x] = level[x]
+            f_ref[o, x] = level[x]
         sum_ref[o] = level[0] + level[1]
         return carry
 
     lax.fori_loop(0, channels, block, 0)
+    save.start()
 
     half_y = cells_y // 2
     modes_c = yc_ref.shape[0] // 2 - half_y
@@ -307,6 +317,7 @@
         return carry
 
     lax.fori_loop(0, coarse_chunks, coarse, 0)
+    save.wait()
 
 
 def widen(matrix_ref, targets):
@@ -373,31 +384,58 @@
     own.wait()
 
 
+class Half:
+    def __init__(self, side, f_hbm, level_hbm, wide_ref, base_hbm, f_ref, level_ref, sem):
+        rows = f_ref.shape[2]
+        at = pl.ds(side * rows, rows)
+        self.loads = [
+            pltpu.make_async_copy(f_hbm.at[:, :, at, :], f_ref, sem.at[0]),
+            pltpu.make_async_copy(level_hbm.at[:, :, at, :], level_ref, sem.at[1]),
+        ]
+        self.save = pltpu.make_async_copy(f_ref, base_hbm, sem.at[2])
+        self.refs = f_ref, level_ref, wide_ref
+
+    def start(self):
+        for load in self.loads:
+            load.start()
+
+    def work(self):
+        f_ref, level_ref, wide_ref = self.refs
+        for load in self.loads:
+            load.wait()
+
+        def block(b, carry):
+            at = pl.ds(pl.multiple_of(b * 8, 8), 8)
+            done = dot_left3(wide_ref[...], load_block(level_ref, at))
+            store_block(f_ref, at, load_block(f_ref, at) + done)
+            return carry
+
+        lax.fori_loop(0, f_ref.shape[2] // 8, block, 0)
+        self.save.start()
+
+
 def coarse_out_kernel(
-    n, tx, in_ref, f_ref, level_ref, wide_ref, out_ref, base_ref, stage, got, send_sem, recv_sem, own_sem
+    n, tx, in_ref, f_hbm, level_hbm, wide_ref, out_ref, base_hbm,
+    stage, got, send_sem, recv_sem, own_sem, f_ref, level_ref, move_sem,
 ):
+    half = Half(0, f_hbm, level_hbm, wide_ref, base_hbm, f_ref, level_ref, move_sem)
+    half.start()
     rows = stage.shape[1]
     for a in range(n):
         stage[a] = in_ref[a * rows : (a + 1) * rows]
     greet(n)
-
-    def work():
-        def block(b, carry):
-            at = pl.ds(pl.multiple_of(b * 8, 8), 8)
-            done = dot_left3(wide_ref[...], load_block(level_ref, at))
-            store_block(base_ref, at, load_block(f_ref, at) + done)
-            return carry
-
-        lax.fori_loop(0, f_ref.shape[2] // 8, block, 0)
-
-    swap(n, stage, got, send_sem, recv_sem, own_sem, work)
+    swap(n, stage, got, send_sem, recv_sem, own_sem, half.work)
     for k in range(out_ref.shape[0]):
         out_ref[k] = sum(got[a] * np.float32(tx[k, a]) for a in range(n))
+    half.save.wait()
 
 
 def coarse_back_kernel(
-    n, tx, in_ref, pooled_ref, wide_ref, out_ref, lifted_ref, stage, got, send_sem, recv_sem, own_sem
+    n, tx, in_ref, f_hbm, level_hbm, proj_ref, pooled_ref, wide_ref, out_ref, base_hbm, lifted_ref,
+    stage, got, send_sem, recv_sem, own_sem, f_ref, level_ref, move_sem,
 ):
+    half = Half(1, f_hbm, level_hbm, proj_ref, base_hbm, f_ref, level_ref, move_sem)
+    half.start()
     rows = stage.shape[1]
     for a in range(n):
         stage[a] = sum(in_ref[k] * np.float32(tx[k, a]) for k in range(in_ref.shape[0]))
@@ -414,24 +452,32 @@
             return carry
 
         lax.fori_loop(0, half_y // 16, block, 0)
+        half.work()
 
     swap(n, stage, got, send_sem, recv_sem, own_sem, work)
     for a in range(n):
         out_ref[a * rows : (a + 1) * rows] = got[a]
+    half.save.wait()
 
 
 def coarse_call(kernel, n, tx, rows, number, shapes, *values):
+    channels, local_x, cells_y, cells_z = values[1].shape
+    part = (channels, local_x, cells_y // 2, cells_z)
+    shapes = (shapes[0], part) + tuple(shapes[1:])
     return pl.pallas_call(
         functools.partial(kernel, n, tx),
         out_shape=tuple(jax.ShapeDtypeStruct(shape, F32) for shape in shapes),
-        in_specs=[whole()] * len(values),
-        out_specs=(whole(),) * len(shapes),
+        in_specs=[whole(), far(), far()] + [whole()] * (len(values) - 3),
+        out_specs=(whole(), far()) + (whole(),) * (len(shapes) - 2),
         scratch_shapes=[
             pltpu.VMEM((n, rows, 128), F32),
             pltpu.VMEM((n, rows, 128), F32),
             pltpu.SemaphoreType.DMA((n,)),
             pltpu.SemaphoreType.DMA((n,)),
             pltpu.SemaphoreType.DMA,
+            pltpu.VMEM(part, F32),
+            pltpu.VMEM(part, F32),
+            pltpu.SemaphoreType.DMA((3,)),
         ],
         compiler_params=pltpu.CompilerParams(collective_id=number, has_side_effects=True),
         name=kernel.__name__,
@@ -439,25 +485,30 @@
 
 
 def mix_kernel(
-    n, tx, wire_ref, w_hbm, f_ref, lift_ref, middle_ref, project_ref,
-    out_ref, lifted_ref, middle_wide, proj_wide, final_wide, lift_wide, got, w_ref, modal, mixed, back,
+    n, tx, wire_ref, w_hbm, f_hbm, lift_ref, middle_ref, project_ref,
+    out_ref, lifted_hbm, middle_wide, proj_wide, final_wide, f_ref, move_sem, lift_wide, got, w_ref, modal, mixed, back,
     send_one, recv_one, send_two, recv_two, own_sem, w_sem,
 ):
     modes_x, channels, _, owned = w_ref.shape
     half = channels // 2
     fetch = pltpu.make_async_copy(w_hbm, w_ref, w_sem)
     fetch.start()
+    load = pltpu.make_async_copy(f_hbm, f_ref, move_sem.at[0])
+    load.start()
+    save = pltpu.make_async_copy(f_ref, lifted_hbm, move_sem.at[1])
     greet(n)
 
     def lift():
         widen(lift_ref, ((lift_wide, 0, same),))
+        load.wait()
 
         def block(b, carry):
             at = pl.ds(pl.multiple_of(b * 8, 8), 8)
-            store_block(lifted_ref, at, dot_left3(lift_wide[...], load_block(f_ref, at)))
+            store_block(f_ref, at, dot_left3(lift_wide[...], load_block(f_ref, at)))
             return carry
 
         lax.fori_loop(0, f_ref.shape[2] // 8, block, 0)
+        save.start()
 
     swap(n, wire_ref, got, send_one, recv_one, own_sem.at[0], lift)
     fetch.wait()
@@ -501,6 +552,7 @@
         )
 
     swap(n, back, out_ref, send_two, recv_two, own_sem.at[1], matrices)
+    save.wait()
 
 
 def mix_fine(wire, weights, features, matrices, tx, n):
@@ -517,9 +569,11 @@
             wide,
             jax.ShapeDtypeStruct((2 * size, 3 * size), BF16),
         ),
-        in_specs=[whole(), pl.BlockSpec(memory_space=pl.ANY)] + [whole()] * 4,
-        out_specs=(whole(),) * 5,
+        in_specs=[whole(), far(), far()] + [whole()] * 3,
+        out_specs=(whole(), far()) + (whole(),) * 3,
         scratch_shapes=[
+            pltpu.VMEM(features.shape, F32),
+            pltpu.SemaphoreType.DMA((2,)),
             pltpu.VMEM(wide.shape, BF16),
             pltpu.VMEM(wire.shape, F32),
             pltpu.VMEM(turned.shape, BF16),
@@ -535,8 +589,16 @@
 
 
 def final_kernel(
-    slab_ref, pooled_ref, base_ref, ty_ref, tz_ref, proj_ref, out_ref, spec_ref
+    slab_ref, pooled_ref, low_hbm, high_hbm, ty_ref, tz_ref, proj_ref, out_hbm,
+    spec_ref, base_ref, load_sem, save_sem,
 ):
+    middle = base_ref.shape[2] // 2
+    loads = [
+        pltpu.make_async_copy(ref, base_ref.at[:, :, pl.ds(side * middle, middle), :], load_sem.at[side])
+        for side, ref in enumerate((low_hbm, high_hbm))
+    ]
+    for load in loads:
+        load.start()
     channels, half_y, _ = pooled_ref.shape
     local_x = base_ref.shape[1]
     modes = ty_ref.shape[1] // 3
@@ -560,22 +622,29 @@
         for h in range(chunks):
             spec_ref[h * per_row + c] = done[h * half_y : (h + 1) * half_y]
 
-    def block(g, carry):
-        at = [pl.ds(pl.multiple_of(g * 16 + 8 * k, 8), 8) for k in range(2)]
+    for load in loads:
+        load.wait()
+    saves = []
+    for g in range(half_y // 16):
+        at = [pl.ds(g * 16 + 8 * k, 8) for k in range(2)]
         pooled = jnp.concatenate([pooled_ref[:, a, :].reshape(channels * 8, 128) for a in at], 1)
         spectral = jnp.concatenate([spec_ref[:, a, :].reshape(channels * 8, 128) for a in at], 1)
-        level = gelu(pooled + spectral)
-        added = dot_left3(proj_ref[...], level)
+        added = dot_left3(proj_ref[...], gelu(pooled + spectral))
         for k in range(2):
             for b in range(2):
                 piece = added[b * channels * 8 : (b + 1) * channels * 8, k * 128 : (k + 1) * 128]
                 piece = piece.reshape(channels, 8, 128)
-                rows = pl.ds(pl.multiple_of(g * 32 + 16 * k + 8 * b, 8), 8)
+                rows = pl.ds(g * 32 + 16 * k + 8 * b, 8)
                 for x in range(local_x):
-                    out_ref[:, x, rows, :] = base_ref[:, x, rows, :] + piece
-        return carry
-
-    lax.fori_loop(0, half_y // 16, block, 0)
+                    base_ref[:, x, rows, :] += piece
+        rows = pl.ds(g * 32, 32)
+        save = pltpu.make_async_copy(
+            base_ref.at[:, :, rows, :], out_hbm.at[:, :, rows, :], save_sem.at[g]
+        )
+        save.start()
+        saves.append(save)
+    for save in saves:
+        save.wait()
 
 
 def on_device(features, fine_weights, middle_weights, lift_fine, lift_middle, project_out):
@@ -631,28 +700,30 @@
             jax.ShapeDtypeStruct((channels, half_y, 128), F32),
             jax.ShapeDtypeStruct((half_ky * parts * chunks_c, 128), F32),
         ),
-        in_specs=[whole()] * 7,
-        out_specs=(whole(), whole(), whole()),
+        in_specs=[whole(), far()] + [whole()] * 5,
+        out_specs=(far(), whole(), whole()),
         scratch_shapes=[
             pltpu.VMEM(features.shape, F32),
             pltpu.VMEM((channels, cells_y, cells_z), F32),
             pltpu.VMEM((KY * local_x * channels, cells_z), F32),
+            pltpu.VMEM(features.shape, F32),
+            pltpu.SemaphoreType.DMA((2,)),
         ],
         name="middle",
     )(slab, lifted, ty_i, tz_i, yc, zc, zp)
 
     count = owned_c // narrow
     rows = count * chunks_c
-    modal, base = coarse_call(
-        coarse_out_kernel, n, txc, rows, 1, ((modes_c, rows, 128), features.shape),
+    modal, base_low = coarse_call(
+        coarse_out_kernel, n, txc, rows, 1, ((modes_c, rows, 128),),
         coarse, features, level, proj,
     )
     modal = modal.reshape(modes_c, count, channels, narrow).transpose(1, 3, 0, 2)
     mixed = mix_modes(modal.reshape(owned_c, modes_c, channels), middle_weights)
     mixed = mixed.reshape(count, narrow, modes_c, channels).transpose(2, 0, 3, 1)
-    slab, lifted = coarse_call(
+    slab, base_high, lifted = coarse_call(
         coarse_back_kernel, n, txc, rows, 2, ((n * rows, 128), pooled.shape),
-        mixed.reshape(modes_c, rows, 128), pooled, liftm,
+        mixed.reshape(modes_c, rows, 128), features, level, proj, pooled, liftm,
     )
 
     tyc_i = left_three(ty_c.T)
@@ -661,11 +732,16 @@
     return pl.pallas_call(
         final_kernel,
         out_shape=jax.ShapeDtypeStruct(features.shape, F32),
-        in_specs=[whole()] * 6,
-        out_specs=whole(),
-        scratch_shapes=[pltpu.VMEM((channels, half_y, 128), F32)],
+        in_specs=[whole(), whole(), far(), far()] + [whole()] * 3,
+        out_specs=far(),
+        scratch_shapes=[
+            pltpu.VMEM((channels, half_y, 128), F32),
+            pltpu.VMEM(features.shape, F32),
+            pltpu.SemaphoreType.DMA((2,)),
+            pltpu.SemaphoreType.DMA((half_y // 16,)),
+        ],
         name="final",
-    )(slab, lifted, base, tyc_i, tzc_i, projm)
+    )(slab, lifted, base_low, base_high, tyc_i, tzc_i, projm)
 
 
 def solution(mesh):

time: 108 us -> 99.6 us (0.922)
  Pallas kernels: 106 us -> 96.6 us
    pallas_call x2, Pallas kernels: 30.7 us -> 27 us  [coarse_call(): pl.pallas_call(functools.partial(kernel, n, tx), out_shape=tuple((jax.Sha...]
    pallas_call x1, Pallas kernels: 36.1 us -> 33.3 us  [mix_fine(): pl.pallas_call(functools.partial(mix_kernel, n, tx), out_shape=(jax.Shape...]
    pallas_call x1, Pallas kernels: 17.2 us -> 15.8 us  [on_device(): pl.pallas_call(middle_kernel, out_shape=(jax.ShapeDtypeStruct(features.sh...]
    pallas_call x1, Pallas kernels: 9 us -> 7.85 us  [on_device(): pl.pallas_call(final_kernel, out_shape=jax.ShapeDtypeStruct(features.shap...]
where the time goes in v3:
time: 99.6 us; the launch traced here: 99.1 us
  Pallas kernels  96.6 us (97%)
  local copies, waits for them, and re-layouts  1.22 us (1%)
    pallas_call x1, Pallas kernels, mix_fine(): pl.pallas_call(functools.partial(mix_kernel, n, tx), out_shape=(jax.Shape...  33.3 us
    pallas_call x2, Pallas kernels, coarse_call(): pl.pallas_call(functools.partial(kernel, n, tx), out_shape=tuple((jax.Sha...  27 us
    pallas_call x1, Pallas kernels, on_device(): pl.pallas_call(middle_kernel, out_shape=(jax.ShapeDtypeStruct(features.sh...  15.8 us
    pallas_call x1, Pallas kernels, forward_fine(): pl.pallas_call(forward_kernel, grid=(channels // block,), out_shape=jax.S...  12.7 us
    pallas_call x1, Pallas kernels, on_device(): pl.pallas_call(final_kernel, out_shape=jax.ShapeDtypeStruct(features.shap...  7.85 us

profile of v3, /device:TPU:0, one launch (start us, length us, event | category | flops | bytes accessed | tf_op | source)
XLA Modules:
  0.0 99.1 jit_solution(7285288846571703050)
XLA Ops:
  0.0 0.0 copy-start
  0.0 12.7 %forward_fine.1.wire_ref = f32[16,72,128]{2,1,0:T(8,128)} custom-call(f32[48,2,96,128]{3,2,1,0:T(8,128)} %f_hbm.5, bf16[96,192]{1,0:T(8,128)(2,1)} %constant.18.clone.ty_ref, bf16[384,128]{1,0:T(8,128)(2,1)} %constant.19.clone.tz_ref), custom_call_target="tpu_custom_call" | custom-call | tf_op jit(solution)/shard_map/forward_fine/pallas_call | solution.py:219
  12.7 33.3 %mix_fine.1 = (f32[16,72,128]{2,1,0:T(8,128)}, f32[48,2,96,128]{3,2,1,0:T(8,128)}, bf16[384,1152]{1,0:T(8,128)(2,1)}, bf16[384,1152]{1,0:T(8,128)(2,1)}, bf16[768,1152]{1,0:T(8,128)(2,1)}) custom-call(f32[16,72,128]{2,1,0:T(8,128)} %forward_fine.1.wire_ref, bf16[8,48,48,96]{3,2,1,0:T(8,128)(2,1)} %bitcast.15, f32[48,2,96,128]{3,2,1,0:T(8,128)} %f_hbm.5, ...), custom_call_target="tpu_custom_call" | custom-call | tf_op jit(solution)/shard_map/mix_fine/pallas_call | solution.py:563
  46.0 15.8 %middle.1 = (f32[48,2,96,128]{3,2,1,0:T(8,128)}, f32[48,48,128]{2,1,0:T(8,128)}, f32[144,128]{1,0:T(8,128)}) custom-call(f32[16,72,128]{2,1,0:T(8,128)} %get-tuple-element.18.slab_ref, f32[48,2,96,128]{3,2,1,0:T(8,128)} %get-tuple-element.19.f_hbm, bf16[96,144]{1,0:T(8,128)(2,1)} %constant.23.clone.ty_ref, bf16[384,128]{1,0:T(8,128)(2,1)} %constant.24.clone.tz_ref, ...), custom_call_target="tpu_custom_call" | custom-call | tf_op jit(solution)/shard_map/middle/pallas_call | solution.py:696
  61.8 15.6 %coarse_out_kernel.1 = (f32[4,9,128]{2,1,0:T(8,128)}, f32[48,2,48,128]{3,2,1,0:T(8,128)}) custom-call(f32[144,128]{1,0:T(8,128)} %get-tuple-element.20.in_ref, f32[48,2,96,128]{3,2,1,0:T(8,128)} %f_hbm.5, f32[48,2,96,128]{3,2,1,0:T(8,128)} %get-tuple-element.21.level_hbm, bf16[384,1152]{1,0:T(8,128)(2,1)} %get-tuple-element.22.wide_ref.proj_ref), custom_call_target="tpu_custom_call" | custom-call | tf_op jit(solution)/shard_map/coarse_out_kernel/pallas_call | solution.py:467
  77.4 0.8 convert_element_type.12
  78.1 0.2 convert_element_type.13
  78.3 0.1 copy.16
  78.4 0.0 copy-done
  78.4 0.4 fusion
  78.9 0.1 copy.17
  79.0 0.8 reshape.11.in_ref
  79.8 11.5 %coarse_back_kernel.1 = (f32[144,128]{1,0:T(8,128)}, f32[48,2,48,128]{3,2,1,0:T(8,128)}, f32[48,48,128]{2,1,0:T(8,128)}) custom-call(f32[4,9,128]{2,1,0:T(8,128)} %reshape.11.in_ref, f32[48,2,96,128]{3,2,1,0:T(8,128)} %f_hbm.5, f32[48,2,96,128]{3,2,1,0:T(8,128)} %get-tuple-element.21.level_hbm, bf16[384,1152]{1,0:T(8,128)(2,1)} %get-tuple-element.22.wide_ref.proj_ref, ...), custom_call_target="tpu_custom_call" | custom-call | tf_op jit(solution)/shard_map/coarse_back_kernel/pallas_call | solution.py:467
  91.3 7.9 %final.1 = f32[48,2,96,128]{3,2,1,0:T(8,128)} custom-call(f32[144,128]{1,0:T(8,128)} %get-tuple-element.26.slab_ref, f32[48,48,128]{2,1,0:T(8,128)} %get-tuple-element.27.pooled_ref, f32[48,2,48,128]{3,2,1,0:T(8,128)} %get-tuple-element.28.low_hbm, f32[48,2,48,128]{3,2,1,0:T(8,128)} %get-tuple-element.29.high_hbm, bf16[48,72]{1,0:T(8,128)(2,1)} %constant.25.clone.ty_ref, ...), custom_call_target="tpu_custom_call" | custom-call | tf_op jit(solution)/shard_map/final/pallas_call | solution.py:732
  (1 shorter events, 0.0 us)
Async XLA Ops:
  0.0 78.4 %copy-start = (bf16[24,4,48,48]{3,2,1,0:T(8,128)(2,1)S(1)}, bf16[24,4,48,48]{3,2,1,0:T(8,128)(2,1)}, u32[]{:S(2)}) copy-start(bf16[24,4,48,48]{3,2,1,0:T(8,128)(2,1)} %param.17) | copy-start | bytes 1327108

commit v4 on v3

--- a/solution.py
+++ b/solution.py
@@ -207,12 +207,12 @@
             out_ref[a] = total
             return carry
 
-        lax.fori_loop(0, n, owner, 0)
+        lax.fori_loop(0, n, owner, 0, unroll=4)
 
 
 def forward_fine(features, modes_y, modes_z, n):
     channels, local_x, cells_y, cells_z = features.shape
-    block = 4
+    block = 8
     ty = left_rows(host_table(modes_y, cells_y))
     tz = right_three(np.tile(host_table(modes_z, cells_z).T, (1, 4)))
     shape = (n, modes_y // n * channels // 2, 128)
@@ -256,7 +256,7 @@
         grown_ref[pl.ds(pl.multiple_of(a * per * rows, 8), per * rows), :] = done
         return carry
 
-    lax.fori_loop(0, n, inverse, 0)
+    lax.fori_loop(0, n, inverse, 0, unroll=4)
 
     def inverse_y(o, carry):
         wide = jnp.concatenate(
@@ -278,7 +278,7 @@
         sum_ref[o] = level[0] + level[1]
         return carry
 
-    lax.fori_loop(0, channels, block, 0)
+    lax.fori_loop(0, channels, block, 0, unroll=2)
     save.start()
 
     half_y = cells_y // 2
@@ -410,7 +410,7 @@
             store_block(f_ref, at, load_block(f_ref, at) + done)
             return carry
 
-        lax.fori_loop(0, f_ref.shape[2] // 8, block, 0)
+        lax.fori_loop(0, f_ref.shape[2] // 8, block, 0, unroll=2)
         self.save.start()
 
 

time: 99.6 us -> 91.8 us (0.922)
  Pallas kernels: 96.6 us -> 88.9 us
    pallas_call x1, Pallas kernels: 12.7 us -> 7.71 us  [forward_fine(): pl.pallas_call(forward_kernel, grid=(channels // block,), out_shape=jax.S...]
    pallas_call x1, Pallas kernels: 15.8 us -> 13.6 us  [on_device(): pl.pallas_call(middle_kernel, out_shape=(jax.ShapeDtypeStruct(features.sh...]
where the time goes in v4:
time: 91.8 us; the launch traced here: 91.4 us
  Pallas kernels  88.9 us (97%)
  local copies, waits for them, and re-layouts  1.22 us (1%)
    pallas_call x1, Pallas kernels, mix_fine(): pl.pallas_call(functools.partial(mix_kernel, n, tx), out_shape=(jax.Shape...  33.3 us
    pallas_call x2, Pallas kernels, coarse_call(): pl.pallas_call(functools.partial(kernel, n, tx), out_shape=tuple((jax.Sha...  26.5 us
    pallas_call x1, Pallas kernels, on_device(): pl.pallas_call(middle_kernel, out_shape=(jax.ShapeDtypeStruct(features.sh...  13.6 us
    pallas_call x1, Pallas kernels, on_device(): pl.pallas_call(final_kernel, out_shape=jax.ShapeDtypeStruct(features.shap...  7.85 us
    pallas_call x1, Pallas kernels, forward_fine(): pl.pallas_call(forward_kernel, grid=(channels // block,), out_shape=jax.S...  7.71 us

profile of v4, /device:TPU:0, one launch (start us, length us, event | category | flops | bytes accessed | tf_op | source)
XLA Modules:
  0.0 91.4 jit_solution(11922911357413049425)
XLA Ops:
  0.0 0.0 copy-start
  0.0 7.7 %forward_fine.1.wire_ref = f32[16,72,128]{2,1,0:T(8,128)} custom-call(f32[48,2,96,128]{3,2,1,0:T(8,128)} %f_hbm.5, bf16[96,192]{1,0:T(8,128)(2,1)} %constant.18.clone.ty_ref, bf16[384,128]{1,0:T(8,128)(2,1)} %constant.19.clone.tz_ref), custom_call_target="tpu_custom_call" | custom-call | tf_op jit(solution)/shard_map/forward_fine/pallas_call | solution.py:219
  7.7 33.3 %mix_fine.1 = (f32[16,72,128]{2,1,0:T(8,128)}, f32[48,2,96,128]{3,2,1,0:T(8,128)}, bf16[384,1152]{1,0:T(8,128)(2,1)}, bf16[384,1152]{1,0:T(8,128)(2,1)}, bf16[768,1152]{1,0:T(8,128)(2,1)}) custom-call(f32[16,72,128]{2,1,0:T(8,128)} %forward_fine.1.wire_ref, bf16[8,48,48,96]{3,2,1,0:T(8,128)(2,1)} %bitcast.15, f32[48,2,96,128]{3,2,1,0:T(8,128)} %f_hbm.5, ...), custom_call_target="tpu_custom_call" | custom-call | tf_op jit(solution)/shard_map/mix_fine/pallas_call | solution.py:563
  41.0 13.6 %middle.1 = (f32[48,2,96,128]{3,2,1,0:T(8,128)}, f32[48,48,128]{2,1,0:T(8,128)}, f32[144,128]{1,0:T(8,128)}) custom-call(f32[16,72,128]{2,1,0:T(8,128)} %get-tuple-element.18.slab_ref, f32[48,2,96,128]{3,2,1,0:T(8,128)} %get-tuple-element.19.f_hbm, bf16[96,144]{1,0:T(8,128)(2,1)} %constant.23.clone.ty_ref, bf16[384,128]{1,0:T(8,128)(2,1)} %constant.24.clone.tz_ref, ...), custom_call_target="tpu_custom_call" | custom-call | tf_op jit(solution)/shard_map/middle/pallas_call | solution.py:696
  54.6 15.1 %coarse_out_kernel.1 = (f32[4,9,128]{2,1,0:T(8,128)}, f32[48,2,48,128]{3,2,1,0:T(8,128)}) custom-call(f32[144,128]{1,0:T(8,128)} %get-tuple-element.20.in_ref, f32[48,2,96,128]{3,2,1,0:T(8,128)} %f_hbm.5, f32[48,2,96,128]{3,2,1,0:T(8,128)} %get-tuple-element.21.level_hbm, bf16[384,1152]{1,0:T(8,128)(2,1)} %get-tuple-element.22.wide_ref.proj_ref), custom_call_target="tpu_custom_call" | custom-call | tf_op jit(solution)/shard_map/coarse_out_kernel/pallas_call | solution.py:467
  69.7 0.8 convert_element_type.12
  70.4 0.2 convert_element_type.13
  70.6 0.1 copy.16
  70.7 0.0 copy-done
  70.7 0.4 fusion
  71.2 0.1 copy.17
  71.3 0.8 reshape.11.in_ref
  72.1 11.4 %coarse_back_kernel.1 = (f32[144,128]{1,0:T(8,128)}, f32[48,2,48,128]{3,2,1,0:T(8,128)}, f32[48,48,128]{2,1,0:T(8,128)}) custom-call(f32[4,9,128]{2,1,0:T(8,128)} %reshape.11.in_ref, f32[48,2,96,128]{3,2,1,0:T(8,128)} %f_hbm.5, f32[48,2,96,128]{3,2,1,0:T(8,128)} %get-tuple-element.21.level_hbm, bf16[384,1152]{1,0:T(8,128)(2,1)} %get-tuple-element.22.wide_ref.proj_ref, ...), custom_call_target="tpu_custom_call" | custom-call | tf_op jit(solution)/shard_map/coarse_back_kernel/pallas_call | solution.py:467
  83.6 7.8 %final.1 = f32[48,2,96,128]{3,2,1,0:T(8,128)} custom-call(f32[144,128]{1,0:T(8,128)} %get-tuple-element.26.slab_ref, f32[48,48,128]{2,1,0:T(8,128)} %get-tuple-element.27.pooled_ref, f32[48,2,48,128]{3,2,1,0:T(8,128)} %get-tuple-element.28.low_hbm, f32[48,2,48,128]{3,2,1,0:T(8,128)} %get-tuple-element.29.high_hbm, bf16[48,72]{1,0:T(8,128)(2,1)} %constant.25.clone.ty_ref, ...), custom_call_target="tpu_custom_call" | custom-call | tf_op jit(solution)/shard_map/final/pallas_call | solution.py:732
  (1 shorter events, 0.0 us)
Async XLA Ops:
  0.0 70.7 %copy-start = (bf16[24,4,48,48]{3,2,1,0:T(8,128)(2,1)S(1)}, bf16[24,4,48,48]{3,2,1,0:T(8,128)(2,1)}, u32[]{:S(2)}) copy-start(bf16[24,4,48,48]{3,2,1,0:T(8,128)(2,1)} %param.17) | copy-start | bytes 1327108

commit v5 on v4

--- a/solution.py
+++ b/solution.py
@@ -207,7 +207,7 @@
             out_ref[a] = total
             return carry
 
-        lax.fori_loop(0, n, owner, 0, unroll=4)
+        lax.fori_loop(0, n, owner, 0, unroll=8)
 
 
 def forward_fine(features, modes_y, modes_z, n):
@@ -256,7 +256,7 @@
         grown_ref[pl.ds(pl.multiple_of(a * per * rows, 8), per * rows), :] = done
         return carry
 
-    lax.fori_loop(0, n, inverse, 0, unroll=4)
+    lax.fori_loop(0, n, inverse, 0, unroll=8)
 
     def inverse_y(o, carry):
         wide = jnp.concatenate(
@@ -267,7 +267,7 @@
             spec_ref[o, x] = done[:, x * cells_z : (x + 1) * cells_z]
         return carry
 
-    lax.fori_loop(0, channels, inverse_y, 0, unroll=4)
+    lax.fori_loop(0, channels, inverse_y, 0, unroll=8)
 
     load.wait()
 
@@ -316,7 +316,7 @@
             ]
         return carry
 
-    lax.fori_loop(0, coarse_chunks, coarse, 0)
+    lax.fori_loop(0, coarse_chunks, coarse, 0, unroll=True)
     save.wait()
 
 
@@ -410,7 +410,7 @@
             store_block(f_ref, at, load_block(f_ref, at) + done)
             return carry
 
-        lax.fori_loop(0, f_ref.shape[2] // 8, block, 0, unroll=2)
+        lax.fori_loop(0, f_ref.shape[2] // 8, block, 0, unroll=3)
         self.save.start()
 
 
@@ -531,7 +531,7 @@
         mixed[k, :, :owned] = total
         return carry
 
-    lax.fori_loop(0, modes_x, mode, 0)
+    lax.fori_loop(0, modes_x, mode, 0, unroll=2)
     wide = lax.broadcasted_iota(jnp.int32, (3 * half, 128), 1)
     for a in range(n):
         first = sum(mixed[k] * np.float32(tx[k, a, 0]) for k in range(modes_x))

time: 91.8 us -> 90.1 us (0.981)
  Pallas kernels: 88.9 us -> 87 us
    pallas_call x1, Pallas kernels: 13.6 us -> 12.2 us  [on_device(): pl.pallas_call(middle_kernel, out_shape=(jax.ShapeDtypeStruct(features.sh...]
where the time goes in v5:
time: 90.1 us; the launch traced here: 89.7 us
  Pallas kernels  87 us (97%)
  local copies, waits for them, and re-layouts  1.22 us (1%)
    pallas_call x1, Pallas kernels, mix_fine(): pl.pallas_call(functools.partial(mix_kernel, n, tx), out_shape=(jax.Shape...  33.1 us
    pallas_call x2, Pallas kernels, coarse_call(): pl.pallas_call(functools.partial(kernel, n, tx), out_shape=tuple((jax.Sha...  26.5 us
    pallas_call x1, Pallas kernels, on_device(): pl.pallas_call(middle_kernel, out_shape=(jax.ShapeDtypeStruct(features.sh...  12.2 us
    pallas_call x1, Pallas kernels, on_device(): pl.pallas_call(final_kernel, out_shape=jax.ShapeDtypeStruct(features.shap...  7.85 us
    pallas_call x1, Pallas kernels, forward_fine(): pl.pallas_call(forward_kernel, grid=(channels // block,), out_shape=jax.S...  7.38 us

profile of v5, /device:TPU:0, one launch (start us, length us, event | category | flops | bytes accessed | tf_op | source)
XLA Modules:
  0.0 89.7 jit_solution(9483670267572618757)
XLA Ops:
  0.0 0.0 copy-start
  0.0 7.4 %forward_fine.1.wire_ref = f32[16,72,128]{2,1,0:T(8,128)} custom-call(f32[48,2,96,128]{3,2,1,0:T(8,128)} %f_hbm.5, bf16[96,192]{1,0:T(8,128)(2,1)} %constant.18.clone.ty_ref, bf16[384,128]{1,0:T(8,128)(2,1)} %constant.19.clone.tz_ref), custom_call_target="tpu_custom_call" | custom-call | tf_op jit(solution)/shard_map/forward_fine/pallas_call | solution.py:219
  7.4 33.1 %mix_fine.1 = (f32[16,72,128]{2,1,0:T(8,128)}, f32[48,2,96,128]{3,2,1,0:T(8,128)}, bf16[384,1152]{1,0:T(8,128)(2,1)}, bf16[384,1152]{1,0:T(8,128)(2,1)}, bf16[768,1152]{1,0:T(8,128)(2,1)}) custom-call(f32[16,72,128]{2,1,0:T(8,128)} %forward_fine.1.wire_ref, bf16[8,48,48,96]{3,2,1,0:T(8,128)(2,1)} %bitcast.15, f32[48,2,96,128]{3,2,1,0:T(8,128)} %f_hbm.5, ...), custom_call_target="tpu_custom_call" | custom-call | tf_op jit(solution)/shard_map/mix_fine/pallas_call | solution.py:563
  40.5 12.2 %middle.1 = (f32[48,2,96,128]{3,2,1,0:T(8,128)}, f32[48,48,128]{2,1,0:T(8,128)}, f32[144,128]{1,0:T(8,128)}) custom-call(f32[16,72,128]{2,1,0:T(8,128)} %get-tuple-element.18.slab_ref, f32[48,2,96,128]{3,2,1,0:T(8,128)} %get-tuple-element.19.f_hbm, bf16[96,144]{1,0:T(8,128)(2,1)} %constant.23.clone.ty_ref, bf16[384,128]{1,0:T(8,128)(2,1)} %constant.24.clone.tz_ref, ...), custom_call_target="tpu_custom_call" | custom-call | tf_op jit(solution)/shard_map/middle/pallas_call | solution.py:696
  52.7 14.9 %coarse_out_kernel.1 = (f32[4,9,128]{2,1,0:T(8,128)}, f32[48,2,48,128]{3,2,1,0:T(8,128)}) custom-call(f32[144,128]{1,0:T(8,128)} %get-tuple-element.20.in_ref, f32[48,2,96,128]{3,2,1,0:T(8,128)} %f_hbm.5, f32[48,2,96,128]{3,2,1,0:T(8,128)} %get-tuple-element.21.level_hbm, bf16[384,1152]{1,0:T(8,128)(2,1)} %get-tuple-element.22.wide_ref.proj_ref), custom_call_target="tpu_custom_call" | custom-call | tf_op jit(solution)/shard_map/coarse_out_kernel/pallas_call | solution.py:467
  67.6 0.8 convert_element_type.12
  68.4 0.2 convert_element_type.13
  68.6 0.1 copy.16
  68.7 0.0 copy-done
  68.7 0.4 fusion
  69.1 0.1 copy.17
  69.3 0.8 reshape.11.in_ref
  70.0 11.6 %coarse_back_kernel.1 = (f32[144,128]{1,0:T(8,128)}, f32[48,2,48,128]{3,2,1,0:T(8,128)}, f32[48,48,128]{2,1,0:T(8,128)}) custom-call(f32[4,9,128]{2,1,0:T(8,128)} %reshape.11.in_ref, f32[48,2,96,128]{3,2,1,0:T(8,128)} %f_hbm.5, f32[48,2,96,128]{3,2,1,0:T(8,128)} %get-tuple-element.21.level_hbm, bf16[384,1152]{1,0:T(8,128)(2,1)} %get-tuple-element.22.wide_ref.proj_ref, ...), custom_call_target="tpu_custom_call" | custom-call | tf_op jit(solution)/shard_map/coarse_back_kernel/pallas_call | solution.py:467
  81.7 7.9 %final.1 = f32[48,2,96,128]{3,2,1,0:T(8,128)} custom-call(f32[144,128]{1,0:T(8,128)} %get-tuple-element.26.slab_ref, f32[48,48,128]{2,1,0:T(8,128)} %get-tuple-element.27.pooled_ref, f32[48,2,48,128]{3,2,1,0:T(8,128)} %get-tuple-element.28.low_hbm, f32[48,2,48,128]{3,2,1,0:T(8,128)} %get-tuple-element.29.high_hbm, bf16[48,72]{1,0:T(8,128)(2,1)} %constant.25.clone.ty_ref, ...), custom_call_target="tpu_custom_call" | custom-call | tf_op jit(solution)/shard_map/final/pallas_call | solution.py:732
  (1 shorter events, 0.0 us)
Async XLA Ops:
  0.0 68.7 %copy-start = (bf16[24,4,48,48]{3,2,1,0:T(8,128)(2,1)S(1)}, bf16[24,4,48,48]{3,2,1,0:T(8,128)(2,1)}, u32[]{:S(2)}) copy-start(bf16[24,4,48,48]{3,2,1,0:T(8,128)(2,1)} %param.17) | copy-start | bytes 1327108
